TPU v7x, 128 devices: a whole 4x4x4 slice. The times are simulated.
128 devices in a mesh: box: 32 (over z, x, core), col: 4 (over y).
Axes of the slice: x: 4, y: 4, z: 4, core: 2. Of those that a mesh axis runs over, the one named last changes fastest.
Arguments:
- density: bfloat16 [4096, 16, 456], P('box'), may hold values from -6 to 6
- export_ids: int32 [32, 32, 4], P('box'), may hold values from -1 to 127, as said below
- list_slot: int32 [4096, 64], P('box'), may hold values from -1 to 127, as said below
- translations: bfloat16 [64, 456, 456], P('col'), may hold values from -0.046875 to 0.046875
- patch_points: int32 [256, 1024], P('box'), may hold values from 0 to 1867775, as said below
- inverses: bfloat16 [256, 1024, 1024], P('box'), may hold values from -0.1875 to 0.1875
Outputs:
- field: bfloat16 [4096, 16, 456], P('box', 'col')
- corrected: bfloat16 [4096, 16, 456], P('box', 'col')
Inputs may be any that keep to these rules, and one draw needn't show every extreme that they name: export_ids[s, d, c] is one of device s's boxes (an index below 128 within s's boxes) or -1 for an empty slot; the boxes of one pair (s, d) are distinct; a device's slots from itself and from the devices just before and after it are all filled. list_slot[b, o] is -1 where box b has no translation o, else an import slot of b's device whose export entry is not -1. `patch_points`: a patch of device d's patches has distinct points within 8 consecutive boxes that begin no more than 2 boxes before d's first box and end no more than 2 boxes after its last.
All inputs are finite; a program needn't handle non-finite values.
Results may differ from a plain program's by a relative error of at most 0.0045.
Values may be sent and summed in bfloat16 or wider, within the bound.
A program may use at most 128 MiB of HBM per device.

v0:
```python
import jax
import jax.numpy as jnp
from jax import lax
from jax.sharding import PartitionSpec as P

RIM = 2


def with_halo(block, sides, width):
    for axis, dim in sides:
        count = lax.axis_size(axis)
        forward = [(i, i + 1) for i in range(count - 1)]
        backward = [(target, source) for source, target in forward]
        low = lax.ppermute(
            lax.slice_in_dim(block, block.shape[dim] - width, None, axis=dim), axis, forward
        )
        high = lax.ppermute(lax.slice_in_dim(block, 0, width, axis=dim), axis, backward)
        block = jnp.concatenate([low, block, high], axis=dim)
    return block


def pick_boxes(columns_first, wanted):
    present = wanted >= 0
    chosen = jnp.take(columns_first, jnp.maximum(wanted, 0), axis=1)
    return jnp.where(present[None, :, None], chosen, jnp.zeros((), chosen.dtype))


def body(density, export_ids, list_slot, translations, patch_points, inverses):
    box_dev, total_cols, width = density.shape
    groups = lax.axis_size("col")
    share = total_cols // groups
    col_index = lax.axis_index("col")
    sources = export_ids.shape[1]
    capacity = export_ids.shape[2]
    wanted = export_ids[0].reshape(-1)
    columns_first = jnp.transpose(density, (1, 0, 2))
    outgoing = pick_boxes(columns_first, wanted).reshape(total_cols, sources, capacity, width)
    imported = lax.all_to_all(outgoing, "box", split_axis=1, concat_axis=1, tiled=True)
    imported = imported.reshape(total_cols, sources * capacity, width)
    local_ops = translations.shape[0]
    slot_columns = lax.dynamic_slice_in_dim(list_slot, col_index * local_ops, local_ops, 1).T
    column_block = imported

    def advance(totals, pieces):
        slot_row, operator = pieces
        live_rows = slot_row >= 0
        gathered = jnp.take(column_block, jnp.maximum(slot_row, 0), axis=1)
        gathered = jnp.where(live_rows[None, :, None], gathered, jnp.zeros((), gathered.dtype))
        term = jnp.dot(
            gathered.reshape(share * lax.axis_size("col") * box_dev, width),
            operator,
            preferred_element_type=jnp.float32,
        )
        return (totals + term.reshape(share * lax.axis_size("col"), box_dev, width), None)

    start_sum = jnp.zeros((share * lax.axis_size("col"), box_dev, width), jnp.float32)
    result, _ = lax.scan(advance, start_sum, (slot_columns, translations))
    field_sum = lax.psum_scatter(result, "col", scatter_dimension=0, tiled=True)
    field_cols = field_sum.astype(jnp.bfloat16)
    extended = with_halo(field_cols, (("box", 1),), RIM)
    flat_field = extended.reshape(share, -1)
    anchor = (lax.axis_index("box") * box_dev - RIM) * width
    local_points = (patch_points - anchor).reshape(-1)
    patch_count = patch_points.shape[0]
    patch_size = patch_points.shape[1]
    values = jnp.take(flat_field, local_points, axis=1).reshape(share, patch_count, patch_size)
    products = jnp.einsum(
        "cpi,pij->cpj", values, inverses, preferred_element_type=jnp.float32
    ).astype(jnp.bfloat16)
    spread = jnp.zeros((share, flat_field.shape[1]), jnp.float32)
    spread = spread.at[:, local_points].add(products.reshape(share, -1).astype(jnp.float32))
    spread = spread.reshape(share, box_dev + 2 * RIM, width)
    returned = with_halo(spread.astype(jnp.bfloat16), (("box", 1),), RIM).astype(spread.dtype)
    owned = spread[:, RIM : RIM + box_dev]
    owned = owned.at[:, :RIM].add(returned[:, :RIM])
    owned = owned.at[:, box_dev - RIM :].add(returned[:, returned.shape[1] - RIM :])
    corrected = (field_cols.astype(jnp.float32) + owned).astype(jnp.bfloat16)
    return (jnp.transpose(field_cols, (1, 0, 2)), jnp.transpose(corrected, (1, 0, 2)))


def solution(mesh):
    return jax.shard_map(
        body,
        mesh=mesh,
        in_specs=(
            P("box", None, None),
            P("box", None, None),
            P("box", None),
            P("col", None, None),
            P("box", None),
            P("box", None, None),
        ),
        out_specs=(P("box", "col", None), P("box", "col", None)),
        check_vma=False,
    )
```

profile of v0, /device:TPU:7, one launch (start us, length us, event | category | flops | bytes accessed | tf_op | source)
XLA Modules:
  0.0 489.7 jit_solution(7884318712816614550)
XLA Ops:
  8.8 4.6 copy.21
  13.6 2.3 gather_fusion.2
  17.6 8.7 %all-to-all-start = ((bf16[16,32,4,456]{3,0,2,1:T(8,128)(2,1)}), bf16[16,32,4,456]{3,0,2,1:T(8,128)(2,1)S(1)}, u32[]{:S(2)}, u32[]{:S(2)}) async-start(bf16[16,32,4,456]{3,0,2,1:T(8,128)(2,1)} %bitcast.49), calls=%async_computation | async-start | bytes 4194304 | tf_op jit(solution)/shard_map/all_to_all | solution.py:38
  26.4 27.5 %all-to-all-done = bf16[16,32,4,456]{3,0,2,1:T(8,128)(2,1)S(1)} async-done(((bf16[16,32,4,456]{3,0,2,1:T(8,128)(2,1)}), bf16[16,32,4,456]{3,0,2,1:T(8,128)(2,1)S(1)}, u32[]{:S(2)}, u32[]{:S(2)}) %all-to-all-start) | async-done | bytes 1867808 | tf_op jit(solution)/shard_map/all_to_all | solution.py:38
  53.9 208.6 %while.13 = (s32[]{:T(128)}, f32[16,128,456]{1,2,0:T(8,128)}, s32[16,128]{1,0:T(8,128)S(1)}, bf16[16,128,456]{2,0,1:T(8,128)(2,1)S(1)}, bf16[16,456,456]{2,1,0:T(8,128)(2,1)}, /*index=5*/s32[]{:T(128)}, s32[]{:T(128)}) while((s32[]{:T(128)}, f32[16,128,456]{1,2,0:T(8,128)}, s32[16,128]{1,0:T(8,128)S(1)}, ...), condition=%wide.region_1.3_spmd.clone, body=%wide.region_0.0_spmd.clone.sunk | while | flops 855443456 | bytes 32456344 | solution.py:57
  55.3 2.3 gather_fusion
  59.3 6.6 %select_add_fusion.2 = f32[16,128,456]{1,2,0:T(8,128)} fusion(f32[16,128,456]{1,2,0:T(8,128)} %get-tuple-element.142, bf16[16,128,456]{2,0,1:T(8,128)(2,1)} %bitcast_select_fusion.3, pred[]{:T(512)S(6)} %compare.14, bf16[16,456,456]{2,1,0:T(8,128)(2,1)} %get-tuple-element.152, s32[]{:T(128)} %get-tuple-element.141), kind=kOutput, calls=%fused_computation.4.clone.1 | convolution fusion | flops 853573632 | bytes 10035713 | tf_op jit(solution)/shard_map/while/body/eval_jaxpr/dot_general | solution.py:49
  67.2 2.3 gather_fusion
  71.3 7.7 %select_add_fusion.2 = f32[16,128,456]{1,2,0:T(8,128)} fusion(f32[16,128,456]{1,2,0:T(8,128)} %get-tuple-element.142, bf16[16,128,456]{2,0,1:T(8,128)(2,1)} %bitcast_select_fusion.3, pred[]{:T(512)S(6)} %compare.14, bf16[16,456,456]{2,1,0:T(8,128)(2,1)} %get-tuple-element.152, s32[]{:T(128)} %get-tuple-element.141), kind=kOutput, calls=%fused_computation.4.clone.1 | convolution fusion | flops 853573632 | bytes 10035713 | tf_op jit(solution)/shard_map/while/body/eval_jaxpr/dot_general | solution.py:49
  80.3 2.3 gather_fusion
  84.4 7.7 %select_add_fusion.2 = f32[16,128,456]{1,2,0:T(8,128)} fusion(f32[16,128,456]{1,2,0:T(8,128)} %get-tuple-element.142, bf16[16,128,456]{2,0,1:T(8,128)(2,1)} %bitcast_select_fusion.3, pred[]{:T(512)S(6)} %compare.14, bf16[16,456,456]{2,1,0:T(8,128)(2,1)} %get-tuple-element.152, s32[]{:T(128)} %get-tuple-element.141), kind=kOutput, calls=%fused_computation.4.clone.1 | convolution fusion | flops 853573632 | bytes 10035713 | tf_op jit(solution)/shard_map/while/body/eval_jaxpr/dot_general | solution.py:49
  93.5 2.3 gather_fusion
  97.5 7.7 %select_add_fusion.2 = f32[16,128,456]{1,2,0:T(8,128)} fusion(f32[16,128,456]{1,2,0:T(8,128)} %get-tuple-element.142, bf16[16,128,456]{2,0,1:T(8,128)(2,1)} %bitcast_select_fusion.3, pred[]{:T(512)S(6)} %compare.14, bf16[16,456,456]{2,1,0:T(8,128)(2,1)} %get-tuple-element.152, s32[]{:T(128)} %get-tuple-element.141), kind=kOutput, calls=%fused_computation.4.clone.1 | convolution fusion | flops 853573632 | bytes 10035713 | tf_op jit(solution)/shard_map/while/body/eval_jaxpr/dot_general | solution.py:49
  106.6 2.3 gather_fusion
  110.6 7.7 %select_add_fusion.2 = f32[16,128,456]{1,2,0:T(8,128)} fusion(f32[16,128,456]{1,2,0:T(8,128)} %get-tuple-element.142, bf16[16,128,456]{2,0,1:T(8,128)(2,1)} %bitcast_select_fusion.3, pred[]{:T(512)S(6)} %compare.14, bf16[16,456,456]{2,1,0:T(8,128)(2,1)} %get-tuple-element.152, s32[]{:T(128)} %get-tuple-element.141), kind=kOutput, calls=%fused_computation.4.clone.1 | convolution fusion | flops 853573632 | bytes 10035713 | tf_op jit(solution)/shard_map/while/body/eval_jaxpr/dot_general | solution.py:49
  119.7 2.3 gather_fusion
  123.7 7.7 %select_add_fusion.2 = f32[16,128,456]{1,2,0:T(8,128)} fusion(f32[16,128,456]{1,2,0:T(8,128)} %get-tuple-element.142, bf16[16,128,456]{2,0,1:T(8,128)(2,1)} %bitcast_select_fusion.3, pred[]{:T(512)S(6)} %compare.14, bf16[16,456,456]{2,1,0:T(8,128)(2,1)} %get-tuple-element.152, s32[]{:T(128)} %get-tuple-element.141), kind=kOutput, calls=%fused_computation.4.clone.1 | convolution fusion | flops 853573632 | bytes 10035713 | tf_op jit(solution)/shard_map/while/body/eval_jaxpr/dot_general | solution.py:49
  132.8 2.3 gather_fusion
  136.8 7.7 %select_add_fusion.2 = f32[16,128,456]{1,2,0:T(8,128)} fusion(f32[16,128,456]{1,2,0:T(8,128)} %get-tuple-element.142, bf16[16,128,456]{2,0,1:T(8,128)(2,1)} %bitcast_select_fusion.3, pred[]{:T(512)S(6)} %compare.14, bf16[16,456,456]{2,1,0:T(8,128)(2,1)} %get-tuple-element.152, s32[]{:T(128)} %get-tuple-element.141), kind=kOutput, calls=%fused_computation.4.clone.1 | convolution fusion | flops 853573632 | bytes 10035713 | tf_op jit(solution)/shard_map/while/body/eval_jaxpr/dot_general | solution.py:49
  145.9 2.3 gather_fusion
  149.9 7.7 %select_add_fusion.2 = f32[16,128,456]{1,2,0:T(8,128)} fusion(f32[16,128,456]{1,2,0:T(8,128)} %get-tuple-element.142, bf16[16,128,456]{2,0,1:T(8,128)(2,1)} %bitcast_select_fusion.3, pred[]{:T(512)S(6)} %compare.14, bf16[16,456,456]{2,1,0:T(8,128)(2,1)} %get-tuple-element.152, s32[]{:T(128)} %get-tuple-element.141), kind=kOutput, calls=%fused_computation.4.clone.1 | convolution fusion | flops 853573632 | bytes 10035713 | tf_op jit(solution)/shard_map/while/body/eval_jaxpr/dot_general | solution.py:49
  159.0 2.3 gather_fusion
  163.0 7.7 %select_add_fusion.2 = f32[16,128,456]{1,2,0:T(8,128)} fusion(f32[16,128,456]{1,2,0:T(8,128)} %get-tuple-element.142, bf16[16,128,456]{2,0,1:T(8,128)(2,1)} %bitcast_select_fusion.3, pred[]{:T(512)S(6)} %compare.14, bf16[16,456,456]{2,1,0:T(8,128)(2,1)} %get-tuple-element.152, s32[]{:T(128)} %get-tuple-element.141), kind=kOutput, calls=%fused_computation.4.clone.1 | convolution fusion | flops 853573632 | bytes 10035713 | tf_op jit(solution)/shard_map/while/body/eval_jaxpr/dot_general | solution.py:49
  172.1 2.3 gather_fusion
  176.1 7.7 %select_add_fusion.2 = f32[16,128,456]{1,2,0:T(8,128)} fusion(f32[16,128,456]{1,2,0:T(8,128)} %get-tuple-element.142, bf16[16,128,456]{2,0,1:T(8,128)(2,1)} %bitcast_select_fusion.3, pred[]{:T(512)S(6)} %compare.14, bf16[16,456,456]{2,1,0:T(8,128)(2,1)} %get-tuple-element.152, s32[]{:T(128)} %get-tuple-element.141), kind=kOutput, calls=%fused_computation.4.clone.1 | convolution fusion | flops 853573632 | bytes 10035713 | tf_op jit(solution)/shard_map/while/body/eval_jaxpr/dot_general | solution.py:49
  185.2 2.3 gather_fusion
  189.3 7.7 %select_add_fusion.2 = f32[16,128,456]{1,2,0:T(8,128)} fusion(f32[16,128,456]{1,2,0:T(8,128)} %get-tuple-element.142, bf16[16,128,456]{2,0,1:T(8,128)(2,1)} %bitcast_select_fusion.3, pred[]{:T(512)S(6)} %compare.14, bf16[16,456,456]{2,1,0:T(8,128)(2,1)} %get-tuple-element.152, s32[]{:T(128)} %get-tuple-element.141), kind=kOutput, calls=%fused_computation.4.clone.1 | convolution fusion | flops 853573632 | bytes 10035713 | tf_op jit(solution)/shard_map/while/body/eval_jaxpr/dot_general | solution.py:49
  198.3 2.3 gather_fusion
  202.4 7.7 %select_add_fusion.2 = f32[16,128,456]{1,2,0:T(8,128)} fusion(f32[16,128,456]{1,2,0:T(8,128)} %get-tuple-element.142, bf16[16,128,456]{2,0,1:T(8,128)(2,1)} %bitcast_select_fusion.3, pred[]{:T(512)S(6)} %compare.14, bf16[16,456,456]{2,1,0:T(8,128)(2,1)} %get-tuple-element.152, s32[]{:T(128)} %get-tuple-element.141), kind=kOutput, calls=%fused_computation.4.clone.1 | convolution fusion | flops 853573632 | bytes 10035713 | tf_op jit(solution)/shard_map/while/body/eval_jaxpr/dot_general | solution.py:49
  211.5 2.3 gather_fusion
  215.5 7.7 %select_add_fusion.2 = f32[16,128,456]{1,2,0:T(8,128)} fusion(f32[16,128,456]{1,2,0:T(8,128)} %get-tuple-element.142, bf16[16,128,456]{2,0,1:T(8,128)(2,1)} %bitcast_select_fusion.3, pred[]{:T(512)S(6)} %compare.14, bf16[16,456,456]{2,1,0:T(8,128)(2,1)} %get-tuple-element.152, s32[]{:T(128)} %get-tuple-element.141), kind=kOutput, calls=%fused_computation.4.clone.1 | convolution fusion | flops 853573632 | bytes 10035713 | tf_op jit(solution)/shard_map/while/body/eval_jaxpr/dot_general | solution.py:49
  228.6 7.7 %select_add_fusion.2 = f32[16,128,456]{1,2,0:T(8,128)} fusion(f32[16,128,456]{1,2,0:T(8,128)} %get-tuple-element.142, bf16[16,128,456]{2,0,1:T(8,128)(2,1)} %bitcast_select_fusion.3, pred[]{:T(512)S(6)} %compare.14, bf16[16,456,456]{2,1,0:T(8,128)(2,1)} %get-tuple-element.152, s32[]{:T(128)} %get-tuple-element.141), kind=kOutput, calls=%fused_computation.4.clone.1 | convolution fusion | flops 853573632 | bytes 10035713 | tf_op jit(solution)/shard_map/while/body/eval_jaxpr/dot_general | solution.py:49
  241.7 7.7 %select_add_fusion.2 = f32[16,128,456]{1,2,0:T(8,128)} fusion(f32[16,128,456]{1,2,0:T(8,128)} %get-tuple-element.142, bf16[16,128,456]{2,0,1:T(8,128)(2,1)} %bitcast_select_fusion.3, pred[]{:T(512)S(6)} %compare.14, bf16[16,456,456]{2,1,0:T(8,128)(2,1)} %get-tuple-element.152, s32[]{:T(128)} %get-tuple-element.141), kind=kOutput, calls=%fused_computation.4.clone.1 | convolution fusion | flops 853573632 | bytes 10035713 | tf_op jit(solution)/shard_map/while/body/eval_jaxpr/dot_general | solution.py:49
  254.8 7.7 %select_add_fusion.2 = f32[16,128,456]{1,2,0:T(8,128)} fusion(f32[16,128,456]{1,2,0:T(8,128)} %get-tuple-element.142, bf16[16,128,456]{2,0,1:T(8,128)(2,1)} %bitcast_select_fusion.3, pred[]{:T(512)S(6)} %compare.14, bf16[16,456,456]{2,1,0:T(8,128)(2,1)} %get-tuple-element.152, s32[]{:T(128)} %get-tuple-element.141), kind=kOutput, calls=%fused_computation.4.clone.1 | convolution fusion | flops 853573632 | bytes 10035713 | tf_op jit(solution)/shard_map/while/body/eval_jaxpr/dot_general | solution.py:49
  263.4 41.7 %reduce-scatter.2.cloned.1.call-done = f32[4,128,456]{1,2,0:T(8,128)} async-done(((f32[16,128,456]{1,2,0:T(8,128)}), f32[4,128,456]{1,2,0:T(8,128)}) %reduce-scatter.2.cloned.1.call-update) | async-done | bytes 933904 | tf_op jit(solution)/shard_map/reduce_scatter | solution.py:58
  306.6 3.8 collective-permute-start
  312.5 3.4 collective-permute-done
  315.9 6.5 %collective-permute-done.1 = bf16[4,2,456]{1,2,0:T(8,128)(2,1)S(1)} collective-permute-done((bf16[4,2,456]{1,2,0:T(8,128)(2,1)S(1)}, bf16[4,2,456]{1,2,0:T(8,128)(2,1)S(1)}, u32[]{:S(2)}, u32[]{:S(2)}) %collective-permute-start.1) | collective-permute-done | bytes 7328 | tf_op jit(solution)/shard_map/ppermute | solution.py:17
  322.9 13.7 %copy.23 = bf16[4,132,456]{0,2,1:T(8,128)(2,1)} copy(bf16[4,132,456]{1,2,0:T(8,128)(2,1)S(1)} %pad_maximum_fusion) | data formatting | bytes 963072 | tf_op jit(solution)/shard_map/concatenate | solution.py:18
  336.6 29.3 %gather_fusion.1 = bf16[8192,4]{1,0:T(8,128)(2,1)S(1)} fusion(bf16[4,60192]{0,1:T(8,128)(2,1)} %bitcast.48, s32[8192]{0:T(1024)S(1)} %broadcast_clamp_fusion), kind=kCustom, calls=%fused_computation.2 | custom fusion | bytes 163840 | tf_op jit(solution)/shard_map/jit(_take)/gather | solution.py:66
  366.8 8.0 %fusion.9 = f32[8,4,1024]{2,1,0:T(4,128)S(1)} fusion(bf16[8,1024,1024]{2,1,0:T(8,128)(2,1)} %param.19, bf16[4,8,1024]{2,0,1:T(4,128)(2,1)S(1)} %copy.24, pred[8,1024]{1,0:T(8,128)(4,1)S(1)} %compare_and_fusion.1), kind=kOutput, calls=%fused_computation.20 | convolution fusion | flops 67207168 | bytes 16982016 | tf_op jit(solution)/shard_map/cpi,pij->cpj/dot_general | solution.py:67
  374.8 2.6 copy.25
  377.4 56.4 %scatter_custom_fusion = f32[4,60192]{0,1:T(8,128)} fusion(s32[8192]{0:T(1024)S(1)} %bitcast.54, f32[8192,4]{1,0:T(8,128)} %copy.25, f32[]{:T(128)} %constant.107.clone.1), kind=kCustom, calls=%fused_computation.16 | custom fusion | flops 32768 | bytes 963584 | tf_op jit(solution)/shard_map/scatter-add | solution.py:71
  433.8 21.7 %copy.26 = f32[4,132,456]{1,2,0:T(8,128)S(1)} copy(f32[4,132,456]{0,2,1:T(8,128)} %bitcast.46) | data formatting | bytes 1926144 | tf_op jit(solution)/shard_map/reshape | solution.py:72
  457.8 2.4 collective-permute-start.3
  463.3 6.5 %collective-permute-done.3 = bf16[4,2,456]{1,2,0:T(8,128)(2,1)S(1)} collective-permute-done((bf16[4,2,456]{1,2,0:T(8,128)(2,1)S(1)}, bf16[4,2,456]{1,2,0:T(8,128)(2,1)S(1)}, u32[]{:S(2)}, u32[]{:S(2)}) %collective-permute-start.3) | collective-permute-done | bytes 7328 | tf_op jit(solution)/shard_map/ppermute | solution.py:17
  472.9 3.4 scatter-add.18
  478.4 3.6 scatter-add.19
  (177 shorter events, 77.2 us)
Async XLA Ops:
  7.2 19.2 %copy-start = (s32[128,64]{0,1:T(8,128)S(1)}, s32[128,64]{0,1:T(8,128)}, u32[]{:S(2)}) copy-start(s32[128,64]{0,1:T(8,128)} %param.16) | copy-start | bytes 98308
  17.6 36.3 %all-to-all-start = ((bf16[16,32,4,456]{3,0,2,1:T(8,128)(2,1)}), bf16[16,32,4,456]{3,0,2,1:T(8,128)(2,1)S(1)}, u32[]{:S(2)}, u32[]{:S(2)}) async-start(bf16[16,32,4,456]{3,0,2,1:T(8,128)(2,1)} %bitcast.49), calls=%async_computation | async-start | bytes 4194304 | tf_op jit(solution)/shard_map/all_to_all | solution.py:38
  26.3 278.8 %reduce-scatter.2.cloned.1.call-start = ((), (), s32[]{:S(2)}) async-start(), calls=%async_computation.2 | async-start | bytes 4669440 | tf_op jit(solution)/shard_map/reduce_scatter | solution.py:58
  53.9 1.4 copy-start.2
  59.3 6.6 %copy-start.3 = (bf16[16,128,456]{2,0,1:T(8,128)(2,1)S(1)}, bf16[16,128,456]{2,0,1:T(8,128)(2,1)}, u32[]{:S(2)}) copy-start(bf16[16,128,456]{2,0,1:T(8,128)(2,1)} %copy-done.2) | copy-start | bytes 5603332 | tf_op jit(solution)/shard_map/while
  65.9 1.4 copy-start.2
  71.3 7.7 %copy-start.3 = (bf16[16,128,456]{2,0,1:T(8,128)(2,1)S(1)}, bf16[16,128,456]{2,0,1:T(8,128)(2,1)}, u32[]{:S(2)}) copy-start(bf16[16,128,456]{2,0,1:T(8,128)(2,1)} %copy-done.2) | copy-start | bytes 5603332 | tf_op jit(solution)/shard_map/while
  79.0 1.4 copy-start.2
  84.4 7.7 %copy-start.3 = (bf16[16,128,456]{2,0,1:T(8,128)(2,1)S(1)}, bf16[16,128,456]{2,0,1:T(8,128)(2,1)}, u32[]{:S(2)}) copy-start(bf16[16,128,456]{2,0,1:T(8,128)(2,1)} %copy-done.2) | copy-start | bytes 5603332 | tf_op jit(solution)/shard_map/while
  92.1 1.4 copy-start.2
  97.5 7.7 %copy-start.3 = (bf16[16,128,456]{2,0,1:T(8,128)(2,1)S(1)}, bf16[16,128,456]{2,0,1:T(8,128)(2,1)}, u32[]{:S(2)}) copy-start(bf16[16,128,456]{2,0,1:T(8,128)(2,1)} %copy-done.2) | copy-start | bytes 5603332 | tf_op jit(solution)/shard_map/while
  105.2 1.4 copy-start.2
  110.6 7.7 %copy-start.3 = (bf16[16,128,456]{2,0,1:T(8,128)(2,1)S(1)}, bf16[16,128,456]{2,0,1:T(8,128)(2,1)}, u32[]{:S(2)}) copy-start(bf16[16,128,456]{2,0,1:T(8,128)(2,1)} %copy-done.2) | copy-start | bytes 5603332 | tf_op jit(solution)/shard_map/while
  118.3 1.4 copy-start.2
  123.7 7.7 %copy-start.3 = (bf16[16,128,456]{2,0,1:T(8,128)(2,1)S(1)}, bf16[16,128,456]{2,0,1:T(8,128)(2,1)}, u32[]{:S(2)}) copy-start(bf16[16,128,456]{2,0,1:T(8,128)(2,1)} %copy-done.2) | copy-start | bytes 5603332 | tf_op jit(solution)/shard_map/while
  131.4 1.4 copy-start.2
  136.8 7.7 %copy-start.3 = (bf16[16,128,456]{2,0,1:T(8,128)(2,1)S(1)}, bf16[16,128,456]{2,0,1:T(8,128)(2,1)}, u32[]{:S(2)}) copy-start(bf16[16,128,456]{2,0,1:T(8,128)(2,1)} %copy-done.2) | copy-start | bytes 5603332 | tf_op jit(solution)/shard_map/while
  144.5 1.4 copy-start.2
  149.9 7.7 %copy-start.3 = (bf16[16,128,456]{2,0,1:T(8,128)(2,1)S(1)}, bf16[16,128,456]{2,0,1:T(8,128)(2,1)}, u32[]{:S(2)}) copy-start(bf16[16,128,456]{2,0,1:T(8,128)(2,1)} %copy-done.2) | copy-start | bytes 5603332 | tf_op jit(solution)/shard_map/while
  157.6 1.4 copy-start.2
  163.0 7.7 %copy-start.3 = (bf16[16,128,456]{2,0,1:T(8,128)(2,1)S(1)}, bf16[16,128,456]{2,0,1:T(8,128)(2,1)}, u32[]{:S(2)}) copy-start(bf16[16,128,456]{2,0,1:T(8,128)(2,1)} %copy-done.2) | copy-start | bytes 5603332 | tf_op jit(solution)/shard_map/while
  170.8 1.4 copy-start.2
  176.1 7.7 %copy-start.3 = (bf16[16,128,456]{2,0,1:T(8,128)(2,1)S(1)}, bf16[16,128,456]{2,0,1:T(8,128)(2,1)}, u32[]{:S(2)}) copy-start(bf16[16,128,456]{2,0,1:T(8,128)(2,1)} %copy-done.2) | copy-start | bytes 5603332 | tf_op jit(solution)/shard_map/while
  183.9 1.4 copy-start.2
  189.3 7.7 %copy-start.3 = (bf16[16,128,456]{2,0,1:T(8,128)(2,1)S(1)}, bf16[16,128,456]{2,0,1:T(8,128)(2,1)}, u32[]{:S(2)}) copy-start(bf16[16,128,456]{2,0,1:T(8,128)(2,1)} %copy-done.2) | copy-start | bytes 5603332 | tf_op jit(solution)/shard_map/while
  197.0 1.4 copy-start.2
  202.4 7.7 %copy-start.3 = (bf16[16,128,456]{2,0,1:T(8,128)(2,1)S(1)}, bf16[16,128,456]{2,0,1:T(8,128)(2,1)}, u32[]{:S(2)}) copy-start(bf16[16,128,456]{2,0,1:T(8,128)(2,1)} %copy-done.2) | copy-start | bytes 5603332 | tf_op jit(solution)/shard_map/while
  210.1 1.4 copy-start.2
  215.5 7.7 %copy-start.3 = (bf16[16,128,456]{2,0,1:T(8,128)(2,1)S(1)}, bf16[16,128,456]{2,0,1:T(8,128)(2,1)}, u32[]{:S(2)}) copy-start(bf16[16,128,456]{2,0,1:T(8,128)(2,1)} %copy-done.2) | copy-start | bytes 5603332 | tf_op jit(solution)/shard_map/while
  223.2 1.4 copy-start.2
  228.6 7.7 %copy-start.3 = (bf16[16,128,456]{2,0,1:T(8,128)(2,1)S(1)}, bf16[16,128,456]{2,0,1:T(8,128)(2,1)}, u32[]{:S(2)}) copy-start(bf16[16,128,456]{2,0,1:T(8,128)(2,1)} %copy-done.2) | copy-start | bytes 5603332 | tf_op jit(solution)/shard_map/while
  236.3 1.4 copy-start.2
  241.7 7.7 %copy-start.3 = (bf16[16,128,456]{2,0,1:T(8,128)(2,1)S(1)}, bf16[16,128,456]{2,0,1:T(8,128)(2,1)}, u32[]{:S(2)}) copy-start(bf16[16,128,456]{2,0,1:T(8,128)(2,1)} %copy-done.2) | copy-start | bytes 5603332 | tf_op jit(solution)/shard_map/while
  249.4 1.4 copy-start.2
  254.8 7.7 %copy-start.3 = (bf16[16,128,456]{2,0,1:T(8,128)(2,1)S(1)}, bf16[16,128,456]{2,0,1:T(8,128)(2,1)}, u32[]{:S(2)}) copy-start(bf16[16,128,456]{2,0,1:T(8,128)(2,1)} %copy-done.2) | copy-start | bytes 5603332 | tf_op jit(solution)/shard_map/while
  262.5 0.8 copy-start.7
  306.6 9.3 %collective-permute-start = (bf16[4,2,456]{1,2,0:T(8,128)(2,1)S(1)}, bf16[4,2,456]{1,2,0:T(8,128)(2,1)S(1)}, u32[]{:S(2)}, u32[]{:S(2)}) collective-permute-start(bf16[4,2,456]{1,2,0:T(8,128)(2,1)S(1)} %get-tuple-element.97), channel_id=1, source_target_pairs={{0,4},{4,8},{8,12},{12,16},{16,20},{20,24},{24,28},{28,32},{32,36}... | collective-permute-start | bytes 21896 | tf_op jit(solution)/shard_map/ppermute | solution.py:14
  310.4 12.0 %collective-permute-start.1 = (bf16[4,2,456]{1,2,0:T(8,128)(2,1)S(1)}, bf16[4,2,456]{1,2,0:T(8,128)(2,1)S(1)}, u32[]{:S(2)}, u32[]{:S(2)}) collective-permute-start(bf16[4,2,456]{1,2,0:T(8,128)(2,1)S(1)} %get-tuple-element.98), channel_id=1, source_target_pairs={{4,0},{8,4},{12,8},{16,12},{20,16},{24,20},{28,24},{32,28},{36,32}... | collective-permute-start | bytes 21896 | tf_op jit(solution)/shard_map/ppermute | solution.py:17
  455.5 4.7 copy-start.4
  455.9 7.4 %collective-permute-start.2 = (bf16[4,2,456]{1,2,0:T(8,128)(2,1)S(1)}, bf16[4,2,456]{1,2,0:T(8,128)(2,1)S(1)}, u32[]{:S(2)}, u32[]{:S(2)}) collective-permute-start(bf16[4,2,456]{1,2,0:T(8,128)(2,1)S(1)} %get-tuple-element.95), channel_id=1, source_target_pairs={{0,4},{4,8},{8,12},{12,16},{16,20},{20,24},{24,28},{28,32},{32,36}... | collective-permute-start | bytes 21896 | tf_op jit(solution)/shard_map/ppermute | solution.py:14
  457.8 12.0 %collective-permute-start.3 = (bf16[4,2,456]{1,2,0:T(8,128)(2,1)S(1)}, bf16[4,2,456]{1,2,0:T(8,128)(2,1)S(1)}, u32[]{:S(2)}, u32[]{:S(2)}) collective-permute-start(bf16[4,2,456]{1,2,0:T(8,128)(2,1)S(1)} %get-tuple-element.96), channel_id=1, source_target_pairs={{4,0},{8,4},{12,8},{16,12},{20,16},{24,20},{28,24},{32,28},{36,32}... | collective-permute-start | bytes 21896 | tf_op jit(solution)/shard_map/ppermute | solution.py:17
  470.4 1.3 copy-start.6
  476.3 2.1 copy-start.5
  476.3 6.6 %copy-start.1 = (s32[128,64]{0,1:T(8,128)S(1)}, s32[128,64]{0,1:T(8,128)}, u32[]{:S(2)}) copy-start(s32[128,64]{0,1:T(8,128)} %param.16) | copy-start | bytes 98308
Sparse Core Ops, SparseCore 0:
  262.7 42.3 reduce-scatter.1
where the time goes:
time: 491 us; the launch traced here: 490 us
  local copies, waits for them, and re-layouts  144 us (29%)
  matrix products  130 us (26%)
  other arithmetic  95.3 us (19%)
  waiting for transfers between devices  86.6 us (18%)
  starting transfers between devices  18.9 us (4%)
  between operations  14.3 us (3%)
    dot_general x16, matrix products, advance(): jnp.dot(gathered.reshape(share * lax.axis_size('col') * box_dev, width),...  122 us
    scatter-add x1, other arithmetic, body(): spread.at[:, local_points]  56.4 us
    reduce_scatter x1, waiting for transfers between devices, body(): field_sum = lax.psum_scatter(result, 'col', scatter_dimension=0, tiled=True)  41.7 us
    gather x16, local copies, waits for them, and re-layouts, advance(): gathered = jnp.take(column_block, jnp.maximum(slot_row, 0), axis=1)  36.3 us
    gather x2, local copies, waits for them, and re-layouts, body(): jnp.take(flat_field, local_points, axis=1)  30.2 us
    select_n x16, other arithmetic, advance(): jnp.where(live_rows[None, :, None], gathered, jnp.zeros((), gathered.dtype))  27.6 us
    all_to_all x1, waiting for transfers between devices, body(): lax.all_to_all(outgoing, 'box', split_axis=1, concat_axis=1, tiled=True)  27.5 us
    reshape x1, local copies, waits for them, and re-layouts, body(): spread = spread.reshape(share, box_dev + 2 * RIM, width)  21.7 us
  transfers between devices with their start and end apart: 6, of which 6 were waited for; matrix products, arithmetic and copies ran while one was open for 0% of the time, Pallas kernels for 0%

commit v1 on v0

v1 whole, which is shorter than its diff:
```python
import functools

import jax
import jax.numpy as jnp
from jax import lax
from jax.experimental import pallas as pl
from jax.experimental.pallas import tpu as pltpu
from jax.sharding import PartitionSpec as P

BF = jnp.bfloat16
F32 = jnp.float32
I32 = jnp.int32
RIM = 2
SPAN = 8
NT = (((1,), (1,)), ((), ()))
TN = (((0,), (0,)), ((), ()))


def dot(a, b):
    return jnp.dot(a, b, preferred_element_type=F32)


def dot_nt(a, b):
    return lax.dot_general(a, b, NT, preferred_element_type=F32)


def iota(shape, axis):
    return lax.broadcasted_iota(I32, shape, axis)


def onehot(mask):
    return jnp.where(mask, 1.0, 0.0).astype(F32)


def kernel(
    sizes,
    dens_hbm, ids_hbm, slot_hbm, trans_hbm, pts_ref, inv_hbm,
    field_ref, corr_ref,
    ids, slots, dens, traw, tpad, inv, stage, outgoing, imp, xbuf, acc, part, recv,
    fown, bhot, halo_out, halo_in, ret_out, ret_in, cacc,
    load_sem, send_sem, recv_sem, rs_send, rs_recv, halo_send, halo_recv,
):
    (ns, cap, cols, width, boxes, groups, nops, chunk, opg) = sizes
    share = cols // groups
    wide = 512
    blocks = wide // 128
    nslot = ns * cap
    me = lax.axis_index("box")
    y = lax.axis_index("col")
    right = lax.rem(me + 1, ns)
    left = lax.rem(me + ns - 1, ns)

    barrier = pltpu.get_barrier_semaphore()

    def greet_box(k, carry):
        pl.semaphore_signal(barrier, inc=1, device_id={"box": lax.rem(me + k, ns)})
        return carry

    lax.fori_loop(1, ns, greet_box, 0)
    for k in range(1, groups):
        pl.semaphore_signal(barrier, inc=1, device_id={"col": lax.rem(y + k, groups)})

    loads = [
        pltpu.make_async_copy(ids_hbm, ids, load_sem.at[0]),
        pltpu.make_async_copy(dens_hbm, dens.at[:, 0:width], load_sem.at[1]),
        pltpu.make_async_copy(
            slot_hbm.at[pl.ds(pl.multiple_of(y * nops, nops), nops)], slots, load_sem.at[2]
        ),
        pltpu.make_async_copy(trans_hbm, traw, load_sem.at[3]),
        pltpu.make_async_copy(inv_hbm, inv, load_sem.at[4]),
    ]
    for load in loads[:4]:
        load.start()

    for c in range(cols):
        dens[c, width:wide, :] = jnp.zeros((wide - width, boxes), BF)
    imp[nslot] = jnp.zeros((cols, wide), BF)

    loads[0].wait()
    rows = []
    sub = iota((8, boxes), 0)
    lane = iota((8, boxes), 1)
    for r in range(nslot // 8):
        picked = jnp.full((8, boxes), -1, I32)
        for j in range(8):
            t = r * 8 + j
            picked = jnp.where(sub == j, ids[t // ns, t % ns], picked)
        rows.append(onehot(lane == picked))
    select = jnp.concatenate(rows, axis=0).astype(BF)

    loads[1].wait()
    for c in range(cols):
        out = dot_nt(select, dens[c])
        for a in range(cap):
            for m in range(blocks):
                stage[m, pl.ds(a * cols + c, ns, stride=cap * cols)] = out[
                    a * ns : (a + 1) * ns, m * 128 : (m + 1) * 128
                ]
    for m in range(blocks):
        outgoing[:, :, m * 128 : (m + 1) * 128] = stage[m].astype(BF).reshape(nslot, cols, 128)

    pl.semaphore_wait(barrier, ns - 1 + groups - 1)

    def exchange(k):
        dst = lax.rem(me + k, ns)
        return pltpu.make_async_remote_copy(
            src_ref=outgoing.at[pl.ds(dst * cap, cap)],
            dst_ref=imp.at[pl.ds(me * cap, cap)],
            send_sem=send_sem.at[k],
            recv_sem=recv_sem.at[k],
            device_id={"box": dst},
        )

    def start_exchange(k, carry):
        exchange(k).start()
        return carry

    lax.fori_loop(1, ns, start_exchange, 0)
    own = pltpu.make_async_copy(
        outgoing.at[pl.ds(me * cap, cap)], imp.at[pl.ds(me * cap, cap)], load_sem.at[5]
    )
    own.start()
    loads[4].start()

    loads[3].wait()

    live = iota((wide, wide - 384), 1) < width - 384

    def pad_operator(o, carry):
        tpad[o, 0:width, 0:width] = traw[o]
        tpad[o, :, 384:] = jnp.where(live, tpad[o, :, 384:], 0.0)
        tpad[o, width:, :] = jnp.zeros((wide - width, wide), BF)
        return carry

    lax.fori_loop(0, nops, pad_operator, 0)

    anchor = (me * boxes - RIM) * width
    local = pts_ref[...] - anchor
    box_of = jnp.floor((local.astype(F32) + 0.5) * (1.0 / width)).astype(I32)
    inner = local - box_of * width
    first = jnp.minimum(jnp.min(box_of, axis=1, keepdims=True), boxes + 2 * RIM - SPAN)
    npatch, psize = pts_ref.shape
    high = jnp.right_shift(inner, 7) * SPAN + (box_of - first)
    low = jnp.bitwise_and(inner, 127)
    sub128 = iota((128, psize), 0)
    for p in range(npatch):
        bhot[p] = onehot(sub128 == low[p : p + 1]).astype(BF)
    firsts = jnp.broadcast_to(first, (npatch, boxes))
    window = [firsts[p : p + 1] + iota((SPAN, boxes), 0) for p in range(npatch)]
    window = jnp.concatenate(window, axis=0)
    lane64 = iota(window.shape, 1)
    pick_own = onehot(window == lane64 + RIM).astype(BF)
    pick_rim = []
    for c in range(share):
        at = jnp.right_shift(lane64, 1)
        odd = jnp.bitwise_and(lane64, 1)
        low_rim = (at == c) & (window == odd)
        high_rim = (at == c + 8) & (window == odd + boxes + RIM)
        pick_rim.append(onehot(low_rim | high_rim).astype(BF)[:, 0:32])

    slots_ready = loads[2]
    slots_ready.wait()
    own.wait()

    def wait_exchange(k, carry):
        exchange(k).wait()
        return carry

    lax.fori_loop(1, ns, wait_exchange, 0)

    nchunk = boxes // chunk

    def send_part(q, k):
        peer = lax.rem(y + k, groups)
        b0 = pl.multiple_of(q * chunk, chunk)
        return pltpu.make_async_remote_copy(
            src_ref=part.at[pl.ds(peer * share, share), pl.ds(b0, chunk)],
            dst_ref=recv.at[k - 1, :, pl.ds(b0, chunk)],
            send_sem=rs_send.at[k - 1, q],
            recv_sem=rs_recv.at[k - 1, q],
            device_id={"col": peer},
        )

    def box_chunk(q, carry):
        acc[...] = jnp.zeros(acc.shape, F32)

        def op_group(g, inner_carry):
            for o in range(opg):
                for j in range(chunk):
                    s = slots[g * opg + o, q * chunk + j]
                    s = jnp.where(s < 0, nslot, s)
                    xbuf[j * cols : (j + 1) * cols, o * wide : (o + 1) * wide] = imp[s]
            weights = tpad[pl.ds(g * opg, opg)].reshape(opg * wide, wide)
            term = dot(xbuf[...], weights)
            for m in range(blocks):
                acc[m] += term[:, m * 128 : (m + 1) * 128]
            return inner_carry

        lax.fori_loop(0, nops // opg, op_group, 0)
        b0 = pl.multiple_of(q * chunk, chunk)
        for c in range(cols):
            for m in range(blocks):
                part[c, pl.ds(b0, chunk), m * 128 : (m + 1) * 128] = acc[
                    m, pl.ds(c, chunk, stride=cols)
                ].astype(BF)
        for k in range(1, groups):
            send_part(q, k).start()
        return carry

    lax.fori_loop(0, nchunk, box_chunk, 0)
    loads[4].wait()

    def wait_part(q, carry):
        for k in range(1, groups):
            send_part(q, k).wait()
        return carry

    lax.fori_loop(0, nchunk, wait_part, 0)

    row16 = iota((16, boxes), 0)
    lane16 = iota((16, boxes), 1)
    rim_low = jnp.zeros((16, wide), F32)
    rim_high = jnp.zeros((16, wide), F32)
    for c in range(share):
        total = part[y * share + c].astype(F32)
        for k in range(groups - 1):
            total = total + recv[k, c].astype(F32)
        fown[c] = total.astype(BF)
        near = (jnp.right_shift(row16, 1) == c)
        odd = jnp.bitwise_and(row16, 1)
        rim_low += dot(onehot(near & (lane16 == odd)).astype(BF), fown[c])
        rim_high += dot(onehot(near & (lane16 == odd + boxes - RIM)).astype(BF), fown[c])
    halo_out[0] = rim_high.astype(BF)
    halo_out[1] = rim_low.astype(BF)

    def swap(source, target, which, index):
        return pltpu.make_async_remote_copy(
            src_ref=source.at[which],
            dst_ref=target.at[which],
            send_sem=halo_send.at[index, which],
            recv_sem=halo_recv.at[index, which],
            device_id={"box": right if which == 0 else left},
        )

    halos = [swap(halo_out, halo_in, w, 0) for w in range(2)]
    for h in halos:
        h.start()
    eye = onehot(iota((width, wide), 0) == iota((width, wide), 1)).astype(BF)
    for c in range(share):
        field_ref[c] = dot_nt(eye, fown[c]).astype(BF)
    for h in halos:
        h.wait()

    rim_rows = halo_in[...].reshape(32, wide)
    windows = [dot(pick_own, fown[c]) + dot(pick_rim[c], rim_rows) for c in range(share)]
    sub_high = iota((blocks * SPAN, psize), 0)
    for p in range(npatch):
        pieces = [
            windows[c][p * SPAN : (p + 1) * SPAN, m * 128 : (m + 1) * 128]
            for c in range(share)
            for m in range(blocks)
        ]
        spread = dot(jnp.concatenate(pieces, axis=0).astype(BF), bhot[p])
        mask = sub_high == high[p : p + 1]
        nrow = blocks * SPAN
        values = [
            jnp.sum(jnp.where(mask, spread[c * nrow : (c + 1) * nrow], 0.0), axis=0, keepdims=True)
            for c in range(share)
        ]
        values = jnp.concatenate(values, axis=0).astype(BF)
        product = dot(values, inv[p]).astype(BF).astype(F32)
        placed = [jnp.where(mask, product[c : c + 1], 0.0) for c in range(share)]
        back = dot_nt(jnp.concatenate(placed, axis=0).astype(BF), bhot[p])
        for c in range(share):
            for m in range(blocks):
                at = c * nrow + m * SPAN
                cacc[c, p * SPAN : (p + 1) * SPAN, m * 128 : (m + 1) * 128] = back[at : at + SPAN]

    rim_sum = jnp.zeros((32, wide), F32)
    for c in range(share):
        rim_sum += lax.dot_general(pick_rim[c], cacc[c].astype(BF), TN, preferred_element_type=F32)
    ret_out[0] = rim_sum[16:32].astype(BF)
    ret_out[1] = rim_sum[0:16].astype(BF)
    returns = [swap(ret_out, ret_in, w, 1) for w in range(2)]
    for h in returns:
        h.start()
    owned = [
        fown[c].astype(F32) + lax.dot_general(pick_own, cacc[c].astype(BF), TN, preferred_element_type=F32)
        for c in range(share)
    ]
    for h in returns:
        h.wait()
    back_rows = ret_in[...].reshape(32, wide)
    for c in range(share):
        boxrow = iota((boxes, 32), 0)
        at = iota((boxes, 32), 1)
        near = jnp.bitwise_and(jnp.right_shift(at, 1), 7) == c
        odd = jnp.bitwise_and(at, 1)
        target = jnp.where(at < 16, odd, odd + boxes - RIM)
        total = owned[c] + dot(onehot(near & (boxrow == target)).astype(BF), back_rows)
        corr_ref[c] = dot_nt(eye, total.astype(BF)).astype(BF)


def body(density, export_ids, list_slot, translations, patch_points, inverses):
    boxes, cols, width = density.shape
    groups = lax.axis_size("col")
    ns, cap = export_ids.shape[1:]
    nops = translations.shape[0]
    npatch, psize = patch_points.shape
    share = cols // groups
    wide = 512
    nslot = ns * cap
    chunk, opg = 32, 4
    sizes = (ns, cap, cols, width, boxes, groups, nops, chunk, opg)
    out = jax.ShapeDtypeStruct((share, width, boxes), BF)
    anyspace = pl.BlockSpec(memory_space=pl.ANY)
    vmem = pl.BlockSpec(memory_space=pltpu.VMEM)
    dma = pltpu.SemaphoreType.DMA
    field, corrected = pl.pallas_call(
        functools.partial(kernel, sizes),
        out_shape=(out, out),
        in_specs=[anyspace, anyspace, anyspace, anyspace, vmem, anyspace],
        out_specs=(vmem, vmem),
        scratch_shapes=[
            pltpu.SMEM((cap, ns), I32),
            pltpu.SMEM((nops, boxes), I32),
            pltpu.VMEM((cols, wide, boxes), BF),
            pltpu.VMEM((nops, width, width), BF),
            pltpu.VMEM((nops, wide, wide), BF),
            pltpu.VMEM((npatch, psize, psize), BF),
            pltpu.VMEM((wide // 128, nslot * cols, 128), F32),
            pltpu.VMEM((nslot, cols, wide), BF),
            pltpu.VMEM((nslot + 1, cols, wide), BF),
            pltpu.VMEM((chunk * cols, opg * wide), BF),
            pltpu.VMEM((wide // 128, chunk * cols, 128), F32),
            pltpu.VMEM((cols, boxes, wide), BF),
            pltpu.VMEM((groups - 1, share, boxes, wide), BF),
            pltpu.VMEM((share, boxes, wide), BF),
            pltpu.VMEM((npatch, 128, psize), BF),
            pltpu.VMEM((2, 16, wide), BF),
            pltpu.VMEM((2, 16, wide), BF),
            pltpu.VMEM((2, 16, wide), BF),
            pltpu.VMEM((2, 16, wide), BF),
            pltpu.VMEM((share, npatch * SPAN, wide), F32),
            dma((6,)),
            dma((ns,)),
            dma((ns,)),
            dma((groups - 1, boxes // chunk)),
            dma((groups - 1, boxes // chunk)),
            dma((2, 2)),
            dma((2, 2)),
        ],
        compiler_params=pltpu.CompilerParams(
            collective_id=0, has_side_effects=True, vmem_limit_bytes=66 * 1000 * 1000
        ),
    )(
        jnp.transpose(density, (1, 2, 0)),
        jnp.transpose(export_ids[0], (1, 0)),
        jnp.transpose(list_slot, (1, 0)),
        translations,
        patch_points,
        inverses,
    )
    return jnp.transpose(field, (2, 0, 1)), jnp.transpose(corrected, (2, 0, 1))


def solution(mesh):
    return jax.shard_map(
        body,
        mesh=mesh,
        in_specs=(
            P("box", None, None),
            P("box", None, None),
            P("box", None),
            P("col", None, None),
            P("box", None),
            P("box", None, None),
        ),
        out_specs=(P("box", "col", None), P("box", "col", None)),
        check_vma=False,
    )
```

time: 491 us -> 92 us (0.19)
  the two profiles are of different devices: /device:TPU:7 before, /device:TPU:0 now
where the time goes in v1:
time: 92 us; the launch traced here: 91.7 us
  Pallas kernels  87.4 us (95%)
  local copies, waits for them, and re-layouts  3.64 us (4%)
    pallas_call x1, Pallas kernels, body(): pl.pallas_call(functools.partial(kernel, sizes), out_shape=(out, out), in...  87.4 us
    unnamed x2, local copies, waits for them, and re-layouts  3.64 us

profile of v1, /device:TPU:0, one launch (start us, length us, event | category | flops | bytes accessed | tf_op | source)
XLA Modules:
  0.0 91.7 jit_solution(12216563146837331413)
XLA Ops:
  0.6 87.4 %shard_map.77 = (bf16[4,456,128]{2,1,0:T(8,128)(2,1)}, bf16[4,456,128]{2,1,0:T(8,128)(2,1)}) custom-call(bf16[16,456,128]{2,1,0:T(8,128)(2,1)} %bitcast.7, s32[4,32]{1,0:T(4,128)} %bitcast.11, s32[64,128]{1,0:T(8,128)} %bitcast.10, bf16[16,456,456]{2,1,0:T(8,128)(2,1)} %trans_hbm.1, s32[8,1024]{1,0:T(8,128)} %pts_ref.1, bf16[8,1024,1024]{2,1,0:T(8,128)(2,1)} %inv_hbm.1), custom_call_target="tpu_custom_call" | custom-call | tf_op jit(solution)/shard_map/pallas_call | solution.py:319
  88.1 1.8 %copy.10 = bf16[128,4,456]{0,2,1:T(8,128)(2,1)} copy(bf16[128,4,456]{0,2,1:T(8,128)(2,1)} %bitcast.9) | data formatting | bytes 933888
  89.9 1.8 %copy.11 = bf16[128,4,456]{0,2,1:T(8,128)(2,1)} copy(bf16[128,4,456]{0,2,1:T(8,128)(2,1)} %bitcast.8) | data formatting | bytes 933888

commit v2 on v1

--- a/solution.py
+++ b/solution.py
@@ -36,9 +36,10 @@
     sizes,
     dens_hbm, ids_hbm, slot_hbm, trans_hbm, pts_ref, inv_hbm,
     field_ref, corr_ref,
-    ids, slots, dens, traw, tpad, inv, stage, outgoing, imp, xbuf, acc, part, recv,
+    ids, slots, dens, traw, tpad, inv, stage, outgoing, imp, xbuf, acc, part, ownp, relay, recv,
     fown, bhot, halo_out, halo_in, ret_out, ret_in, cacc,
-    load_sem, send_sem, recv_sem, rs_send, rs_recv, halo_send, halo_recv,
+    load_sem, send_sem, recv_sem, pass_send, pass_recv, rel_send, rel_recv, rs_send, rs_recv,
+    halo_send, halo_recv,
 ):
     (ns, cap, cols, width, boxes, groups, nops, chunk, opg) = sizes
     share = cols // groups
@@ -98,41 +99,6 @@
                 ]
     for m in range(blocks):
         outgoing[:, :, m * 128 : (m + 1) * 128] = stage[m].astype(BF).reshape(nslot, cols, 128)
-
-    pl.semaphore_wait(barrier, ns - 1 + groups - 1)
-
-    def exchange(k):
-        dst = lax.rem(me + k, ns)
-        return pltpu.make_async_remote_copy(
-            src_ref=outgoing.at[pl.ds(dst * cap, cap)],
-            dst_ref=imp.at[pl.ds(me * cap, cap)],
-            send_sem=send_sem.at[k],
-            recv_sem=recv_sem.at[k],
-            device_id={"box": dst},
-        )
-
-    def start_exchange(k, carry):
-        exchange(k).start()
-        return carry
-
-    lax.fori_loop(1, ns, start_exchange, 0)
-    own = pltpu.make_async_copy(
-        outgoing.at[pl.ds(me * cap, cap)], imp.at[pl.ds(me * cap, cap)], load_sem.at[5]
-    )
-    own.start()
-    loads[4].start()
-
-    loads[3].wait()
-
-    live = iota((wide, wide - 384), 1) < width - 384
-
-    def pad_operator(o, carry):
-        tpad[o, 0:width, 0:width] = traw[o]
-        tpad[o, :, 384:] = jnp.where(live, tpad[o, :, 384:], 0.0)
-        tpad[o, width:, :] = jnp.zeros((wide - width, wide), BF)
-        return carry
-
-    lax.fori_loop(0, nops, pad_operator, 0)
 
     anchor = (me * boxes - RIM) * width
     local = pts_ref[...] - anchor
@@ -158,30 +124,160 @@
         high_rim = (at == c + 8) & (window == odd + boxes + RIM)
         pick_rim.append(onehot(low_rim | high_rim).astype(BF)[:, 0:32])
 
-    slots_ready = loads[2]
-    slots_ready.wait()
+    pl.semaphore_wait(barrier, ns - 1 + groups - 1)
+
+    first_cap = 2 * lax.rem(y, 2)
+
+    def exchange(k):
+        dst = lax.rem(me + k, ns)
+        return pltpu.make_async_remote_copy(
+            src_ref=outgoing.at[pl.ds(dst * cap + first_cap, 2)],
+            dst_ref=imp.at[pl.ds(me * cap + first_cap, 2)],
+            send_sem=send_sem.at[k],
+            recv_sem=recv_sem.at[k],
+            device_id={"box": dst},
+        )
+
+    def start_exchange(k, carry):
+        exchange(k).start()
+        return carry
+
+    lax.fori_loop(1, ns, start_exchange, 0)
+    own = pltpu.make_async_copy(
+        outgoing.at[pl.ds(me * cap, cap)], imp.at[pl.ds(me * cap, cap)], load_sem.at[5]
+    )
+    own.start()
+    loads[4].start()
+    loads[3].wait()
+
+    col_up = lax.rem(y + 1, groups)
+    col_down = lax.rem(y + groups - 1, groups)
+
+    def pass_on(k, way):
+        at = lax.rem(me + ns - k, ns) * cap + first_cap + way
+        return pltpu.make_async_remote_copy(
+            src_ref=imp.at[at],
+            dst_ref=imp.at[at],
+            send_sem=pass_send.at[way, k],
+            recv_sem=pass_recv.at[way, k],
+            device_id={"col": col_down if way == 0 else col_up},
+        )
+
+    live = iota((wide, wide - 384), 1) < width - 384
+
+    def pad_operator(o):
+        tpad[o, 0:width, 0:width] = traw[o]
+        tpad[o, :, 384:] = jnp.where(live, tpad[o, :, 384:], 0.0)
+        tpad[o, width:, :] = jnp.zeros((wide - width, wide), BF)
+
+    def relay_boxes(k):
+        exchange(k).wait_recv()
+        pass_on(k, 0).start()
+        pass_on(k, 1).start()
+
+    def relay_and_pad(o, carry):
+        pad_operator(o)
+        relay_boxes(2 * o + 1)
+        relay_boxes(2 * o + 2)
+        return carry
+
+    lax.fori_loop(0, nops - 1, relay_and_pad, 0)
+    pad_operator(nops - 1)
+    relay_boxes(ns - 1)
+
+    loads[2].wait()
     own.wait()
 
     def wait_exchange(k, carry):
-        exchange(k).wait()
+        exchange(k).wait_send()
+        pass_on(k, 0).wait()
+        pass_on(k, 1).wait()
         return carry
 
     lax.fori_loop(1, ns, wait_exchange, 0)
 
     nchunk = boxes // chunk
-
-    def send_part(q, k):
-        peer = lax.rem(y + k, groups)
-        b0 = pl.multiple_of(q * chunk, chunk)
+    half = chunk // 2
+    opposite = lax.rem(y + 2, groups)
+    towards = (col_up, col_down)
+
+    def turn(i):
+        return lax.rem(i + nchunk - 1, nchunk)
+
+    def send_relay(i, way):
+        q = turn(i)
         return pltpu.make_async_remote_copy(
-            src_ref=part.at[pl.ds(peer * share, share), pl.ds(b0, chunk)],
-            dst_ref=recv.at[k - 1, :, pl.ds(b0, chunk)],
-            send_sem=rs_send.at[k - 1, q],
-            recv_sem=rs_recv.at[k - 1, q],
-            device_id={"col": peer},
+            src_ref=part.at[
+                pl.ds(opposite * share, share), pl.ds(pl.multiple_of(q * chunk + way * half, half), half)
+            ],
+            dst_ref=relay.at[way, :, pl.ds(pl.multiple_of(q * half, half), half)],
+            send_sem=rel_send.at[way, i],
+            recv_sem=rel_recv.at[way, i],
+            device_id={"col": towards[way]},
         )
 
-    def box_chunk(q, carry):
+    def send_part(i, way):
+        b0 = pl.multiple_of(turn(i) * chunk, chunk)
+        return pltpu.make_async_remote_copy(
+            src_ref=part.at[pl.ds(towards[way] * share, share), pl.ds(b0, chunk)],
+            dst_ref=recv.at[way, :, pl.ds(b0, chunk)],
+            send_sem=rs_send.at[way, i],
+            recv_sem=rs_recv.at[way, i],
+            device_id={"col": towards[way]},
+        )
+
+    def combine(i):
+        q = turn(i)
+        for way in range(2):
+            send_relay(i, way).wait()
+            b0 = pl.multiple_of(q * chunk + way * half, half)
+            r0 = pl.multiple_of(q * half, half)
+            for c in range(share):
+                mine = part[towards[way] * share + c, pl.ds(b0, half)].astype(F32)
+                mine = mine + relay[way, c, pl.ds(r0, half)].astype(F32)
+                part[towards[way] * share + c, pl.ds(b0, half)] = mine.astype(BF)
+            send_part(i, way).start()
+
+    def wait_part(i):
+        for way in range(2):
+            send_part(i, way).wait()
+
+    def summed(c, b0, count):
+        total = ownp[c, b0 : b0 + count]
+        for way in range(2):
+            total = total + recv[way, c, b0 : b0 + count].astype(F32)
+        return total.astype(BF)
+
+    def swap(source, target, which, index):
+        return pltpu.make_async_remote_copy(
+            src_ref=source.at[which],
+            dst_ref=target.at[which],
+            send_sem=halo_send.at[index, which],
+            recv_sem=halo_recv.at[index, which],
+            device_id={"box": right if which == 0 else left},
+        )
+
+    halos = [swap(halo_out, halo_in, w, 0) for w in range(2)]
+
+    def send_rims():
+        wait_part(0)
+        wait_part(1)
+        row16 = iota((16, 16), 0)
+        lane16 = iota((16, 16), 1)
+        odd = jnp.bitwise_and(row16, 1)
+        rim_low = jnp.zeros((16, wide), F32)
+        rim_high = jnp.zeros((16, wide), F32)
+        for c in range(share):
+            near = jnp.right_shift(row16, 1) == c
+            rim_low += dot(onehot(near & (lane16 == odd)).astype(BF), summed(c, 0, 16))
+            rim_high += dot(onehot(near & (lane16 == odd + 16 - RIM)).astype(BF), summed(c, boxes - 16, 16))
+        halo_out[0] = rim_high.astype(BF)
+        halo_out[1] = rim_low.astype(BF)
+        for h in halos:
+            h.start()
+
+    def box_chunk(i, carry):
+        q = turn(i)
         acc[...] = jnp.zeros(acc.shape, F32)
 
         def op_group(g, inner_carry):
@@ -198,56 +294,33 @@
 
         lax.fori_loop(0, nops // opg, op_group, 0)
         b0 = pl.multiple_of(q * chunk, chunk)
-        for c in range(cols):
-            for m in range(blocks):
-                part[c, pl.ds(b0, chunk), m * 128 : (m + 1) * 128] = acc[
-                    m, pl.ds(c, chunk, stride=cols)
-                ].astype(BF)
-        for k in range(1, groups):
-            send_part(q, k).start()
+        for m in range(blocks):
+            span = slice(m * 128, (m + 1) * 128)
+            for c in range(cols):
+                part[c, pl.ds(b0, chunk), span] = acc[m, pl.ds(c, chunk, stride=cols)].astype(BF)
+            for c in range(share):
+                ownp[c, pl.ds(b0, chunk), span] = acc[m, pl.ds(y * share + c, chunk, stride=cols)]
+        for way in range(2):
+            send_relay(i, way).start()
+
+        @pl.when(i >= 1)
+        def _():
+            combine(i - 1)
+
+        @pl.when(i == nchunk - 1)
+        def _():
+            send_rims()
+
         return carry
 
     lax.fori_loop(0, nchunk, box_chunk, 0)
+    combine(nchunk - 1)
     loads[4].wait()
-
-    def wait_part(q, carry):
-        for k in range(1, groups):
-            send_part(q, k).wait()
-        return carry
-
-    lax.fori_loop(0, nchunk, wait_part, 0)
-
-    row16 = iota((16, boxes), 0)
-    lane16 = iota((16, boxes), 1)
-    rim_low = jnp.zeros((16, wide), F32)
-    rim_high = jnp.zeros((16, wide), F32)
+    for i in range(2, nchunk):
+        wait_part(i)
+
     for c in range(share):
-        total = part[y * share + c].astype(F32)
-        for k in range(groups - 1):
-            total = total + recv[k, c].astype(F32)
-        fown[c] = total.astype(BF)
-        near = (jnp.right_shift(row16, 1) == c)
-        odd = jnp.bitwise_and(row16, 1)
-        rim_low += dot(onehot(near & (lane16 == odd)).astype(BF), fown[c])
-        rim_high += dot(onehot(near & (lane16 == odd + boxes - RIM)).astype(BF), fown[c])
-    halo_out[0] = rim_high.astype(BF)
-    halo_out[1] = rim_low.astype(BF)
-
-    def swap(source, target, which, index):
-        return pltpu.make_async_remote_copy(
-            src_ref=source.at[which],
-            dst_ref=target.at[which],
-            send_sem=halo_send.at[index, which],
-            recv_sem=halo_recv.at[index, which],
-            device_id={"box": right if which == 0 else left},
-        )
-
-    halos = [swap(halo_out, halo_in, w, 0) for w in range(2)]
-    for h in halos:
-        h.start()
-    eye = onehot(iota((width, wide), 0) == iota((width, wide), 1)).astype(BF)
-    for c in range(share):
-        field_ref[c] = dot_nt(eye, fown[c]).astype(BF)
+        fown[c] = summed(c, 0, boxes)
     for h in halos:
         h.wait()
 
@@ -284,6 +357,9 @@
     returns = [swap(ret_out, ret_in, w, 1) for w in range(2)]
     for h in returns:
         h.start()
+    eye = onehot(iota((width, wide), 0) == iota((width, wide), 1)).astype(BF)
+    for c in range(share):
+        field_ref[c] = dot_nt(eye, fown[c]).astype(BF)
     owned = [
         fown[c].astype(F32) + lax.dot_general(pick_own, cacc[c].astype(BF), TN, preferred_element_type=F32)
         for c in range(share)
@@ -334,7 +410,9 @@
             pltpu.VMEM((chunk * cols, opg * wide), BF),
             pltpu.VMEM((wide // 128, chunk * cols, 128), F32),
             pltpu.VMEM((cols, boxes, wide), BF),
-            pltpu.VMEM((groups - 1, share, boxes, wide), BF),
+            pltpu.VMEM((share, boxes, wide), F32),
+            pltpu.VMEM((2, share, boxes // 2, wide), BF),
+            pltpu.VMEM((2, share, boxes, wide), BF),
             pltpu.VMEM((share, boxes, wide), BF),
             pltpu.VMEM((npatch, 128, psize), BF),
             pltpu.VMEM((2, 16, wide), BF),
@@ -345,8 +423,12 @@
             dma((6,)),
             dma((ns,)),
             dma((ns,)),
-            dma((groups - 1, boxes // chunk)),
-            dma((groups - 1, boxes // chunk)),
+            dma((2, ns)),
+            dma((2, ns)),
+            dma((2, boxes // chunk)),
+            dma((2, boxes // chunk)),
+            dma((2, boxes // chunk)),
+            dma((2, boxes // chunk)),
             dma((2, 2)),
             dma((2, 2)),
         ],

time: 92 us -> 84.7 us (0.921)
  the two profiles are of different devices: /device:TPU:0 before, /device:TPU:1 now
where the time goes in v2:
time: 84.7 us; the launch traced here: 84.4 us
  Pallas kernels  80.1 us (95%)
  local copies, waits for them, and re-layouts  3.64 us (4%)
    pallas_call x1, Pallas kernels, body(): pl.pallas_call(functools.partial(kernel, sizes), out_shape=(out, out), in...  80.1 us
    unnamed x2, local copies, waits for them, and re-layouts  3.64 us

profile of v2, /device:TPU:1, one launch (start us, length us, event | category | flops | bytes accessed | tf_op | source)
XLA Modules:
  0.0 84.4 jit_solution(14453176219488900507)
XLA Ops:
  0.6 80.1 %shard_map.77 = (bf16[4,456,128]{2,1,0:T(8,128)(2,1)}, bf16[4,456,128]{2,1,0:T(8,128)(2,1)}) custom-call(bf16[16,456,128]{2,1,0:T(8,128)(2,1)} %bitcast.7, s32[4,32]{1,0:T(4,128)} %bitcast.11, s32[64,128]{1,0:T(8,128)} %bitcast.10, bf16[16,456,456]{2,1,0:T(8,128)(2,1)} %trans_hbm.1, s32[8,1024]{1,0:T(8,128)} %pts_ref.1, bf16[8,1024,1024]{2,1,0:T(8,128)(2,1)} %inv_hbm.1), custom_call_target="tpu_custom_call" | custom-call | tf_op jit(solution)/shard_map/pallas_call | solution.py:395
  80.7 1.8 %copy.10 = bf16[128,4,456]{0,2,1:T(8,128)(2,1)} copy(bf16[128,4,456]{0,2,1:T(8,128)(2,1)} %bitcast.9) | data formatting | bytes 933888
  82.6 1.8 %copy.11 = bf16[128,4,456]{0,2,1:T(8,128)(2,1)} copy(bf16[128,4,456]{0,2,1:T(8,128)(2,1)} %bitcast.8) | data formatting | bytes 933888

commit v3 on v2

--- a/solution.py
+++ b/solution.py
@@ -128,21 +128,29 @@
 
     first_cap = 2 * lax.rem(y, 2)
 
-    def exchange(k):
-        dst = lax.rem(me + k, ns)
+    def shifted(k, sign):
+        z = lax.rem(me // 8 + sign * (k // 8) + 4, 4)
+        x = lax.rem(lax.rem(me // 2, 4) + sign * lax.rem(k // 2, 4) + 4, 4)
+        core = lax.rem(lax.rem(me, 2) + lax.rem(k, 2), 2)
+        return z * 8 + x * 2 + core
+
+    def exchange(j):
+        k = lax.rem(j * 11, ns)
+        dst = shifted(k, 1)
         return pltpu.make_async_remote_copy(
             src_ref=outgoing.at[pl.ds(dst * cap + first_cap, 2)],
             dst_ref=imp.at[pl.ds(me * cap + first_cap, 2)],
-            send_sem=send_sem.at[k],
-            recv_sem=recv_sem.at[k],
+            send_sem=send_sem.at[j],
+            recv_sem=recv_sem.at[j],
             device_id={"box": dst},
         )
 
-    def start_exchange(k, carry):
-        exchange(k).start()
+    def start_exchange(j, carry):
+        exchange(j).start()
         return carry
 
-    lax.fori_loop(1, ns, start_exchange, 0)
+    ahead = 31
+    lax.fori_loop(1, 1 + ahead, start_exchange, 0)
     own = pltpu.make_async_copy(
         outgoing.at[pl.ds(me * cap, cap)], imp.at[pl.ds(me * cap, cap)], load_sem.at[5]
     )
@@ -154,7 +162,7 @@
     col_down = lax.rem(y + groups - 1, groups)
 
     def pass_on(k, way):
-        at = lax.rem(me + ns - k, ns) * cap + first_cap + way
+        at = shifted(lax.rem(k * 11, ns), -1) * cap + first_cap + way
         return pltpu.make_async_remote_copy(
             src_ref=imp.at[at],
             dst_ref=imp.at[at],
@@ -171,9 +179,13 @@
         tpad[o, width:, :] = jnp.zeros((wide - width, wide), BF)
 
     def relay_boxes(k):
-        exchange(k).wait_recv()
+        exchange(k).wait()
         pass_on(k, 0).start()
         pass_on(k, 1).start()
+
+        @pl.when(k + ahead < ns)
+        def _():
+            exchange(k + ahead).start()
 
     def relay_and_pad(o, carry):
         pad_operator(o)
@@ -189,7 +201,6 @@
     own.wait()
 
     def wait_exchange(k, carry):
-        exchange(k).wait_send()
         pass_on(k, 0).wait()
         pass_on(k, 1).wait()
         return carry

time: 84.7 us -> 79.5 us (0.939)
  Pallas kernels: 80.1 us -> 75 us
    pallas_call x1, Pallas kernels: 80.1 us -> 75 us  [body(): pl.pallas_call(functools.partial(kernel, sizes), out_shape=(out, out), in...]
where the time goes in v3:
time: 79.5 us; the launch traced here: 79.3 us
  Pallas kernels  75 us (94%)
  local copies, waits for them, and re-layouts  3.64 us (5%)
    pallas_call x1, Pallas kernels, body(): pl.pallas_call(functools.partial(kernel, sizes), out_shape=(out, out), in...  75 us
    unnamed x2, local copies, waits for them, and re-layouts  3.64 us

profile of v3, /device:TPU:1, one launch (start us, length us, event | category | flops | bytes accessed | tf_op | source)
XLA Modules:
  0.0 79.3 jit_solution(10661350492996475304)
XLA Ops:
  0.6 75.0 %shard_map.77 = (bf16[4,456,128]{2,1,0:T(8,128)(2,1)}, bf16[4,456,128]{2,1,0:T(8,128)(2,1)}) custom-call(bf16[16,456,128]{2,1,0:T(8,128)(2,1)} %bitcast.7, s32[4,32]{1,0:T(4,128)} %bitcast.11, s32[64,128]{1,0:T(8,128)} %bitcast.10, bf16[16,456,456]{2,1,0:T(8,128)(2,1)} %trans_hbm.1, s32[8,1024]{1,0:T(8,128)} %pts_ref.1, bf16[8,1024,1024]{2,1,0:T(8,128)(2,1)} %inv_hbm.1), custom_call_target="tpu_custom_call" | custom-call | tf_op jit(solution)/shard_map/pallas_call | solution.py:406
  75.6 1.8 %copy.10 = bf16[128,4,456]{0,2,1:T(8,128)(2,1)} copy(bf16[128,4,456]{0,2,1:T(8,128)(2,1)} %bitcast.9) | data formatting | bytes 933888
  77.5 1.8 %copy.11 = bf16[128,4,456]{0,2,1:T(8,128)(2,1)} copy(bf16[128,4,456]{0,2,1:T(8,128)(2,1)} %bitcast.8) | data formatting | bytes 933888

commit v4 on v2

--- a/solution.py
+++ b/solution.py
@@ -36,7 +36,7 @@
     sizes,
     dens_hbm, ids_hbm, slot_hbm, trans_hbm, pts_ref, inv_hbm,
     field_ref, corr_ref,
-    ids, slots, dens, traw, tpad, inv, stage, outgoing, imp, xbuf, acc, part, ownp, relay, recv,
+    ids, slots, dens, traw, tpad, inv, stage, outgoing, imp0, imp1, xbuf, xbuf2, acc, part, ownp, relay, recv,
     fown, bhot, halo_out, halo_in, ret_out, ret_in, cacc,
     load_sem, send_sem, recv_sem, pass_send, pass_recv, rel_send, rel_recv, rs_send, rs_recv,
     halo_send, halo_recv,
@@ -46,6 +46,7 @@
     wide = 512
     blocks = wide // 128
     nslot = ns * cap
+    lot = cols // 2
     me = lax.axis_index("box")
     y = lax.axis_index("col")
     right = lax.rem(me + 1, ns)
@@ -75,7 +76,9 @@
 
     for c in range(cols):
         dens[c, width:wide, :] = jnp.zeros((wide - width, boxes), BF)
-    imp[nslot] = jnp.zeros((cols, wide), BF)
+    imps = (imp0, imp1)
+    for imp in imps:
+        imp[nslot] = jnp.zeros((lot, wide), BF)
 
     loads[0].wait()
     rows = []
@@ -94,11 +97,12 @@
         out = dot_nt(select, dens[c])
         for a in range(cap):
             for m in range(blocks):
-                stage[m, pl.ds(a * cols + c, ns, stride=cap * cols)] = out[
+                row = (c % share // 2) * nslot * lot + a * lot + c // share * 2 + c % 2
+                stage[m, pl.ds(row, ns, stride=cap * lot)] = out[
                     a * ns : (a + 1) * ns, m * 128 : (m + 1) * 128
                 ]
     for m in range(blocks):
-        outgoing[:, :, m * 128 : (m + 1) * 128] = stage[m].astype(BF).reshape(nslot, cols, 128)
+        outgoing[:, :, :, m * 128 : (m + 1) * 128] = stage[m].astype(BF).reshape(2, nslot, lot, 128)
 
     anchor = (me * boxes - RIM) * width
     local = pts_ref[...] - anchor
@@ -128,38 +132,49 @@
 
     first_cap = 2 * lax.rem(y, 2)
 
-    def exchange(k):
-        dst = lax.rem(me + k, ns)
+    z, x, core = me // 8, lax.rem(me // 2, 4), lax.rem(me, 2)
+    z_at = [lax.rem(z + d, 4) * 8 for d in range(4)]
+    x_at = [lax.rem(x + d, 4) * 2 for d in range(4)]
+    core_at = [core, 1 - core]
+
+    def shifted(j, sign):
+        k = j * 11 % ns
+        return z_at[sign * (k // 8) % 4] + x_at[sign * (k // 2 % 4) % 4] + core_at[k % 2]
+
+    def exchange(h, j):
+        dst = shifted(j, 1)
         return pltpu.make_async_remote_copy(
-            src_ref=outgoing.at[pl.ds(dst * cap + first_cap, 2)],
-            dst_ref=imp.at[pl.ds(me * cap + first_cap, 2)],
-            send_sem=send_sem.at[k],
-            recv_sem=recv_sem.at[k],
+            src_ref=outgoing.at[h, pl.ds(dst * cap + first_cap, 2)],
+            dst_ref=imps[h].at[pl.ds(me * cap + first_cap, 2)],
+            send_sem=send_sem.at[h],
+            recv_sem=recv_sem.at[h, j],
             device_id={"box": dst},
         )
 
-    def start_exchange(k, carry):
-        exchange(k).start()
-        return carry
-
-    lax.fori_loop(1, ns, start_exchange, 0)
-    own = pltpu.make_async_copy(
-        outgoing.at[pl.ds(me * cap, cap)], imp.at[pl.ds(me * cap, cap)], load_sem.at[5]
-    )
-    own.start()
+    for h in range(2):
+        for j in range(1, ns):
+            exchange(h, j).start()
+    owns = [
+        pltpu.make_async_copy(
+            outgoing.at[h, pl.ds(me * cap, cap)], imps[h].at[pl.ds(me * cap, cap)], load_sem.at[5 + h]
+        )
+        for h in range(2)
+    ]
+    for own in owns:
+        own.start()
     loads[4].start()
     loads[3].wait()
 
     col_up = lax.rem(y + 1, groups)
     col_down = lax.rem(y + groups - 1, groups)
 
-    def pass_on(k, way):
-        at = lax.rem(me + ns - k, ns) * cap + first_cap + way
+    def pass_on(h, k, way):
+        at = shifted(k, -1) * cap + first_cap + way
         return pltpu.make_async_remote_copy(
-            src_ref=imp.at[at],
-            dst_ref=imp.at[at],
-            send_sem=pass_send.at[way, k],
-            recv_sem=pass_recv.at[way, k],
+            src_ref=imps[h].at[at],
+            dst_ref=imps[h].at[at],
+            send_sem=pass_send.at[h, way],
+            recv_sem=pass_recv.at[h, way],
             device_id={"col": col_down if way == 0 else col_up},
         )
 
@@ -170,83 +185,88 @@
         tpad[o, :, 384:] = jnp.where(live, tpad[o, :, 384:], 0.0)
         tpad[o, width:, :] = jnp.zeros((wide - width, wide), BF)
 
-    def relay_boxes(k):
-        exchange(k).wait_recv()
-        pass_on(k, 0).start()
-        pass_on(k, 1).start()
-
-    def relay_and_pad(o, carry):
+    def relay_boxes(h, k):
+        exchange(h, k).wait_recv()
+        pass_on(h, k, 0).start()
+        pass_on(h, k, 1).start()
+
+    def pad_some(o, carry):
         pad_operator(o)
-        relay_boxes(2 * o + 1)
-        relay_boxes(2 * o + 2)
         return carry
 
-    lax.fori_loop(0, nops - 1, relay_and_pad, 0)
-    pad_operator(nops - 1)
-    relay_boxes(ns - 1)
+    lax.fori_loop(0, nops // 2, pad_some, 0)
+    for j in range(1, ns):
+        relay_boxes(0, j)
+        if j in (9, 17):
+            lax.fori_loop(nops // 2 + (j - 9) // 2, nops // 2 + (j - 9) // 2 + nops // 4, pad_some, 0)
 
     loads[2].wait()
-    own.wait()
-
-    def wait_exchange(k, carry):
-        exchange(k).wait_send()
-        pass_on(k, 0).wait()
-        pass_on(k, 1).wait()
-        return carry
-
-    lax.fori_loop(1, ns, wait_exchange, 0)
+    for own in owns:
+        own.wait()
+
+    def wait_passed(h):
+        some = imps[h].at[0 : ns - 1]
+        more = imps[h].at[0 : 2 * (ns - 1)]
+        for way in range(2):
+            pltpu.make_async_copy(some, some, pass_send.at[h, way]).wait()
+            pltpu.make_async_copy(some, some, pass_recv.at[h, way]).wait()
+        pltpu.make_async_copy(more, more, send_sem.at[h]).wait()
+
+    wait_passed(0)
 
     nchunk = boxes // chunk
+    nstep = 2 * nchunk
     half = chunk // 2
+    relays = 8
     opposite = lax.rem(y + 2, groups)
     towards = (col_up, col_down)
 
     def turn(i):
-        return lax.rem(i + nchunk - 1, nchunk)
+        return i // nchunk, lax.rem(i + nchunk - 1, nchunk)
+
+    def place(i):
+        h, q = turn(i)
+        return h * nchunk + q
 
     def send_relay(i, way):
-        q = turn(i)
+        q = place(i)
         return pltpu.make_async_remote_copy(
-            src_ref=part.at[
-                pl.ds(opposite * share, share), pl.ds(pl.multiple_of(q * chunk + way * half, half), half)
-            ],
-            dst_ref=relay.at[way, :, pl.ds(pl.multiple_of(q * half, half), half)],
+            src_ref=part.at[opposite, q, way],
+            dst_ref=relay.at[way, q],
             send_sem=rel_send.at[way, i],
             recv_sem=rel_recv.at[way, i],
             device_id={"col": towards[way]},
         )
 
     def send_part(i, way):
-        b0 = pl.multiple_of(turn(i) * chunk, chunk)
+        q = place(i)
         return pltpu.make_async_remote_copy(
-            src_ref=part.at[pl.ds(towards[way] * share, share), pl.ds(b0, chunk)],
-            dst_ref=recv.at[way, :, pl.ds(b0, chunk)],
+            src_ref=part.at[towards[way], q],
+            dst_ref=recv.at[way, q],
             send_sem=rs_send.at[way, i],
             recv_sem=rs_recv.at[way, i],
             device_id={"col": towards[way]},
         )
 
     def combine(i):
-        q = turn(i)
+        q = place(i)
         for way in range(2):
             send_relay(i, way).wait()
-            b0 = pl.multiple_of(q * chunk + way * half, half)
-            r0 = pl.multiple_of(q * half, half)
-            for c in range(share):
-                mine = part[towards[way] * share + c, pl.ds(b0, half)].astype(F32)
-                mine = mine + relay[way, c, pl.ds(r0, half)].astype(F32)
-                part[towards[way] * share + c, pl.ds(b0, half)] = mine.astype(BF)
+            for c in range(share // 2):
+                mine = part[towards[way], q, way, c].astype(F32) + relay[way, q, c].astype(F32)
+                part[towards[way], q, way, c] = mine.astype(BF)
             send_part(i, way).start()
 
     def wait_part(i):
         for way in range(2):
             send_part(i, way).wait()
 
-    def summed(c, b0, count):
-        total = ownp[c, b0 : b0 + count]
+    def summed(c, q, h):
+        b0 = q * chunk + h * half
+        total = ownp[c, b0 : b0 + half]
         for way in range(2):
-            total = total + recv[way, c, b0 : b0 + count].astype(F32)
-        return total.astype(BF)
+            total = total + recv[way, c // 2 * nchunk + q, h, c % 2].astype(F32)
+        return total
 
     def swap(source, target, which, index):
         return pltpu.make_async_remote_copy(
@@ -260,46 +280,66 @@
     halos = [swap(halo_out, halo_in, w, 0) for w in range(2)]
 
     def send_rims():
-        wait_part(0)
-        wait_part(1)
-        row16 = iota((16, 16), 0)
-        lane16 = iota((16, 16), 1)
+        for i in (0, 1, nchunk, nchunk + 1):
+            wait_part(i)
+        row16 = iota((16, half), 0)
+        lane16 = iota((16, half), 1)
         odd = jnp.bitwise_and(row16, 1)
         rim_low = jnp.zeros((16, wide), F32)
         rim_high = jnp.zeros((16, wide), F32)
         for c in range(share):
             near = jnp.right_shift(row16, 1) == c
-            rim_low += dot(onehot(near & (lane16 == odd)).astype(BF), summed(c, 0, 16))
-            rim_high += dot(onehot(near & (lane16 == odd + 16 - RIM)).astype(BF), summed(c, boxes - 16, 16))
+            rim_low += dot(onehot(near & (lane16 == odd)).astype(BF), summed(c, 0, 0).astype(BF))
+            rim_high += dot(onehot(near & (lane16 == odd + half - RIM)).astype(BF), summed(c, nchunk - 1, 1).astype(BF))
         halo_out[0] = rim_high.astype(BF)
         halo_out[1] = rim_low.astype(BF)
         for h in halos:
             h.start()
 
-    def box_chunk(i, carry):
-        q = turn(i)
-        acc[...] = jnp.zeros(acc.shape, F32)
-
-        def op_group(g, inner_carry):
-            for o in range(opg):
-                for j in range(chunk):
-                    s = slots[g * opg + o, q * chunk + j]
-                    s = jnp.where(s < 0, nslot, s)
-                    xbuf[j * cols : (j + 1) * cols, o * wide : (o + 1) * wide] = imp[s]
-            weights = tpad[pl.ds(g * opg, opg)].reshape(opg * wide, wide)
-            term = dot(xbuf[...], weights)
-            for m in range(blocks):
-                acc[m] += term[:, m * 128 : (m + 1) * 128]
-            return inner_carry
-
-        lax.fori_loop(0, nops // opg, op_group, 0)
+    def gather(h, i, g, into):
+        q = turn(i)[1]
+        for o in range(opg):
+            for j in range(chunk):
+                s = slots[g * opg + o, q * chunk + j]
+                s = jnp.where(s < 0, nslot, s)
+                into[j * lot : (j + 1) * lot, o * wide : (o + 1) * wide] = imps[h][s]
+
+    def weights(g):
+        return tpad[g * opg : (g + 1) * opg].reshape(opg * wide, wide)
+
+    def relay_later(i, slot):
+        for step in range(-(-(ns - 1) // (2 * relays))):
+
+            @pl.when(i == step)
+            def _():
+                first = (2 * step + slot) * relays + 1
+                for k in range(first, min(first + relays, ns)):
+                    relay_boxes(1, k)
+
+    def box_chunk(h, i):
+        q = turn(i)[1]
+        gather(h, i, 1, xbuf2)
+        term = dot(xbuf[...], weights(0))
+        for m in range(blocks):
+            acc[m] = term[:, m * 128 : (m + 1) * 128]
+        if h == 0:
+            relay_later(i, 0)
+        gather(h, i + 1, 0, xbuf)
+        term = dot(xbuf2[...], weights(1))
+        for m in range(blocks):
+            acc[m] += term[:, m * 128 : (m + 1) * 128]
+        if h == 0:
+            relay_later(i, 1)
         b0 = pl.multiple_of(q * chunk, chunk)
+        at = place(i)
         for m in range(blocks):
             span = slice(m * 128, (m + 1) * 128)
-            for c in range(cols):
-                part[c, pl.ds(b0, chunk), span] = acc[m, pl.ds(c, chunk, stride=cols)].astype(BF)
-            for c in range(share):
-                ownp[c, pl.ds(b0, chunk), span] = acc[m, pl.ds(y * share + c, chunk, stride=cols)]
+            for r in range(lot):
+                for b in range(2):
+                    mine = acc[m, pl.ds(b * half * lot + r, half, stride=lot)]
+                    part[r // 2, at, b, r % 2, :, span] = mine.astype(BF)
+            for r in range(2):
+                ownp[2 * h + r, pl.ds(b0, chunk), span] = acc[m, pl.ds(y * 2 + r, chunk, stride=lot)]
         for way in range(2):
             send_relay(i, way).start()
 
@@ -307,20 +347,32 @@
         def _():
             combine(i - 1)
 
-        @pl.when(i == nchunk - 1)
+        @pl.when(i == nstep - 1)
         def _():
             send_rims()
 
+    def first_half(i, carry):
+        box_chunk(0, i)
         return carry
 
-    lax.fori_loop(0, nchunk, box_chunk, 0)
-    combine(nchunk - 1)
+    def second_half(i, carry):
+        box_chunk(1, i)
+        return carry
+
+    gather(0, 0, 0, xbuf)
+    lax.fori_loop(0, nchunk, first_half, 0)
+    wait_passed(1)
+    gather(1, nchunk, 0, xbuf)
+    lax.fori_loop(nchunk, nstep, second_half, 0)
+    combine(nstep - 1)
     loads[4].wait()
-    for i in range(2, nchunk):
-        wait_part(i)
+    for h in range(2):
+        for i in range(2, nchunk):
+            wait_part(h * nchunk + i)
 
     for c in range(share):
-        fown[c] = summed(c, 0, boxes)
+        pieces = [summed(c, q, h) for q in range(nchunk) for h in range(2)]
+        fown[c] = jnp.concatenate(pieces, axis=0).astype(BF)
     for h in halos:
         h.wait()
 
@@ -386,7 +438,8 @@
     share = cols // groups
     wide = 512
     nslot = ns * cap
-    chunk, opg = 32, 4
+    chunk, opg = 32, 8
+    nchunk = boxes // chunk
     sizes = (ns, cap, cols, width, boxes, groups, nops, chunk, opg)
     out = jax.ShapeDtypeStruct((share, width, boxes), BF)
     anyspace = pl.BlockSpec(memory_space=pl.ANY)
@@ -405,14 +458,16 @@
             pltpu.VMEM((nops, wide, wide), BF),
             pltpu.VMEM((npatch, psize, psize), BF),
             pltpu.VMEM((wide // 128, nslot * cols, 128), F32),
-            pltpu.VMEM((nslot, cols, wide), BF),
-            pltpu.VMEM((nslot + 1, cols, wide), BF),
-            pltpu.VMEM((chunk * cols, opg * wide), BF),
-            pltpu.VMEM((wide // 128, chunk * cols, 128), F32),
-            pltpu.VMEM((cols, boxes, wide), BF),
+            pltpu.VMEM((2, nslot, cols // 2, wide), BF),
+            pltpu.VMEM((nslot + 1, cols // 2, wide), BF),
+            pltpu.VMEM((nslot + 1, cols // 2, wide), BF),
+            pltpu.VMEM((chunk * cols // 2, opg * wide), BF),
+            pltpu.VMEM((chunk * cols // 2, opg * wide), BF),
+            pltpu.VMEM((wide // 128, chunk * cols // 2, 128), F32),
+            pltpu.VMEM((groups, 2 * nchunk, 2, share // 2, chunk // 2, wide), BF),
             pltpu.VMEM((share, boxes, wide), F32),
-            pltpu.VMEM((2, share, boxes // 2, wide), BF),
-            pltpu.VMEM((2, share, boxes, wide), BF),
+            pltpu.VMEM((2, 2 * nchunk, share // 2, chunk // 2, wide), BF),
+            pltpu.VMEM((2, 2 * nchunk, 2, share // 2, chunk // 2, wide), BF),
             pltpu.VMEM((share, boxes, wide), BF),
             pltpu.VMEM((npatch, 128, psize), BF),
             pltpu.VMEM((2, 16, wide), BF),
@@ -420,15 +475,15 @@
             pltpu.VMEM((2, 16, wide), BF),
             pltpu.VMEM((2, 16, wide), BF),
             pltpu.VMEM((share, npatch * SPAN, wide), F32),
-            dma((6,)),
-            dma((ns,)),
-            dma((ns,)),
+            dma((7,)),
+            dma((2,)),
             dma((2, ns)),
-            dma((2, ns)),
-            dma((2, boxes // chunk)),
-            dma((2, boxes // chunk)),
-            dma((2, boxes // chunk)),
-            dma((2, boxes // chunk)),
+            dma((2, 2)),
+            dma((2, 2)),
+            dma((2, 2 * nchunk)),
+            dma((2, 2 * nchunk)),
+            dma((2, 2 * nchunk)),
+            dma((2, 2 * nchunk)),
             dma((2, 2)),
             dma((2, 2)),
         ],

time: 84.7 us -> 75.2 us (0.89)
  the two profiles are of different devices: /device:TPU:1 before, /device:TPU:0 now
where the time goes in v4:
time: 75.2 us; the launch traced here: 74.9 us
  Pallas kernels  70.6 us (94%)
  local copies, waits for them, and re-layouts  3.64 us (5%)
    pallas_call x1, Pallas kernels, body(): pl.pallas_call(functools.partial(kernel, sizes), out_shape=(out, out), in...  70.6 us
    unnamed x2, local copies, waits for them, and re-layouts  3.64 us

profile of v4, /device:TPU:0, one launch (start us, length us, event | category | flops | bytes accessed | tf_op | source)
XLA Modules:
  0.0 74.9 jit_solution(9615184449265524460)
XLA Ops:
  0.6 70.6 %shard_map.77 = (bf16[4,456,128]{2,1,0:T(8,128)(2,1)}, bf16[4,456,128]{2,1,0:T(8,128)(2,1)}) custom-call(bf16[16,456,128]{2,1,0:T(8,128)(2,1)} %bitcast.7, s32[4,32]{1,0:T(4,128)} %bitcast.11, s32[64,128]{1,0:T(8,128)} %bitcast.10, bf16[16,456,456]{2,1,0:T(8,128)(2,1)} %trans_hbm.1, s32[8,1024]{1,0:T(8,128)} %pts_ref.1, bf16[8,1024,1024]{2,1,0:T(8,128)(2,1)} %inv_hbm.1), custom_call_target="tpu_custom_call" | custom-call | tf_op jit(solution)/shard_map/pallas_call | solution.py:448
  71.3 1.8 %copy.10 = bf16[128,4,456]{0,2,1:T(8,128)(2,1)} copy(bf16[128,4,456]{0,2,1:T(8,128)(2,1)} %bitcast.9) | data formatting | bytes 933888
  73.1 1.8 %copy.11 = bf16[128,4,456]{0,2,1:T(8,128)(2,1)} copy(bf16[128,4,456]{0,2,1:T(8,128)(2,1)} %bitcast.8) | data formatting | bytes 933888

commit v5 on v4

--- a/solution.py
+++ b/solution.py
@@ -104,6 +104,41 @@
     for m in range(blocks):
         outgoing[:, :, :, m * 128 : (m + 1) * 128] = stage[m].astype(BF).reshape(2, nslot, lot, 128)
 
+    pl.semaphore_wait(barrier, ns - 1 + groups - 1)
+
+    first_cap = 2 * lax.rem(y, 2)
+
+    z, x, core = me // 8, lax.rem(me // 2, 4), lax.rem(me, 2)
+    z_at = [lax.rem(z + d, 4) * 8 for d in range(4)]
+    x_at = [lax.rem(x + d, 4) * 2 for d in range(4)]
+    core_at = [core, 1 - core]
+
+    def shifted(j, sign):
+        k = j * 11 % ns
+        return z_at[sign * (k // 8) % 4] + x_at[sign * (k // 2 % 4) % 4] + core_at[k % 2]
+
+    def exchange(h, j):
+        dst = shifted(j, 1)
+        return pltpu.make_async_remote_copy(
+            src_ref=outgoing.at[h, pl.ds(dst * cap + first_cap, 2)],
+            dst_ref=imps[h].at[pl.ds(me * cap + first_cap, 2)],
+            send_sem=send_sem.at[h],
+            recv_sem=recv_sem.at[h, j],
+            device_id={"box": dst},
+        )
+
+    for h in range(2):
+        for j in range(1, ns):
+            exchange(h, j).start()
+    owns = [
+        pltpu.make_async_copy(
+            outgoing.at[h, pl.ds(me * cap, cap)], imps[h].at[pl.ds(me * cap, cap)], load_sem.at[5 + h]
+        )
+        for h in range(2)
+    ]
+    for own in owns:
+        own.start()
+    loads[4].start()
     anchor = (me * boxes - RIM) * width
     local = pts_ref[...] - anchor
     box_of = jnp.floor((local.astype(F32) + 0.5) * (1.0 / width)).astype(I32)
@@ -128,41 +163,6 @@
         high_rim = (at == c + 8) & (window == odd + boxes + RIM)
         pick_rim.append(onehot(low_rim | high_rim).astype(BF)[:, 0:32])
 
-    pl.semaphore_wait(barrier, ns - 1 + groups - 1)
-
-    first_cap = 2 * lax.rem(y, 2)
-
-    z, x, core = me // 8, lax.rem(me // 2, 4), lax.rem(me, 2)
-    z_at = [lax.rem(z + d, 4) * 8 for d in range(4)]
-    x_at = [lax.rem(x + d, 4) * 2 for d in range(4)]
-    core_at = [core, 1 - core]
-
-    def shifted(j, sign):
-        k = j * 11 % ns
-        return z_at[sign * (k // 8) % 4] + x_at[sign * (k // 2 % 4) % 4] + core_at[k % 2]
-
-    def exchange(h, j):
-        dst = shifted(j, 1)
-        return pltpu.make_async_remote_copy(
-            src_ref=outgoing.at[h, pl.ds(dst * cap + first_cap, 2)],
-            dst_ref=imps[h].at[pl.ds(me * cap + first_cap, 2)],
-            send_sem=send_sem.at[h],
-            recv_sem=recv_sem.at[h, j],
-            device_id={"box": dst},
-        )
-
-    for h in range(2):
-        for j in range(1, ns):
-            exchange(h, j).start()
-    owns = [
-        pltpu.make_async_copy(
-            outgoing.at[h, pl.ds(me * cap, cap)], imps[h].at[pl.ds(me * cap, cap)], load_sem.at[5 + h]
-        )
-        for h in range(2)
-    ]
-    for own in owns:
-        own.start()
-    loads[4].start()
     loads[3].wait()
 
     col_up = lax.rem(y + 1, groups)
@@ -427,6 +427,17 @@
         target = jnp.where(at < 16, odd, odd + boxes - RIM)
         total = owned[c] + dot(onehot(near & (boxrow == target)).astype(BF), back_rows)
         corr_ref[c] = dot_nt(eye, total.astype(BF)).astype(BF)
+
+
+def hand_over(field_ref, corr_ref, field_out, corr_out, sem):
+    copies = [
+        pltpu.make_async_copy(field_ref, field_out, sem.at[0]),
+        pltpu.make_async_copy(corr_ref, corr_out, sem.at[1]),
+    ]
+    for copy in copies:
+        copy.start()
+    for copy in copies:
+        copy.wait()
 
 
 def body(density, export_ids, list_slot, translations, patch_points, inverses):
@@ -498,6 +509,13 @@
         patch_points,
         inverses,
     )
+    field, corrected = pl.pallas_call(
+        hand_over,
+        out_shape=(out, out),
+        in_specs=[vmem, vmem],
+        out_specs=(anyspace, anyspace),
+        scratch_shapes=[dma((2,))],
+    )(field, corrected)
     return jnp.transpose(field, (2, 0, 1)), jnp.transpose(corrected, (2, 0, 1))
 
 

time: 75.2 us -> 73.1 us (0.972)
  local copies, waits for them, and re-layouts: 3.64 us -> 0 us
  Pallas kernels: 70.6 us -> 72.1 us
    unnamed x2 -> x0, local copies, waits for them, and re-layouts: 3.64 us -> none
    pallas_call x0 -> x1, Pallas kernels: none -> 2.1 us  [body(): pl.pallas_call(hand_over, out_shape=(out, out), in_specs=[vmem, vmem], ou...]
where the time goes in v5:
time: 73.1 us; the launch traced here: 72.9 us
  Pallas kernels  72.1 us (99%)
  between operations  0.8 us (1%)
    pallas_call x1, Pallas kernels, body(): pl.pallas_call(functools.partial(kernel, sizes), out_shape=(out, out), in...  70 us
    pallas_call x1, Pallas kernels, body(): pl.pallas_call(hand_over, out_shape=(out, out), in_specs=[vmem, vmem], ou...  2.1 us

profile of v5, /device:TPU:0, one launch (start us, length us, event | category | flops | bytes accessed | tf_op | source)
XLA Modules:
  0.0 72.9 jit_solution(2559270674464237839)
XLA Ops:
  0.6 70.0 %shard_map.77 = (bf16[4,456,128]{2,1,0:T(8,128)(2,1)}, bf16[4,456,128]{2,1,0:T(8,128)(2,1)}) custom-call(bf16[16,456,128]{2,1,0:T(8,128)(2,1)} %bitcast.7, s32[4,32]{1,0:T(4,128)} %bitcast.9, s32[64,128]{1,0:T(8,128)} %bitcast.8, bf16[16,456,456]{2,1,0:T(8,128)(2,1)} %trans_hbm.1, s32[8,1024]{1,0:T(8,128)} %pts_ref.1, bf16[8,1024,1024]{2,1,0:T(8,128)(2,1)} %inv_hbm.1), custom_call_target="tpu_custom_call" | custom-call | tf_op jit(solution)/shard_map/pallas_call | solution.py:459
  70.6 2.1 %shard_map.78 = (bf16[4,456,128]{2,1,0:T(8,128)(2,1)}, bf16[4,456,128]{2,1,0:T(8,128)(2,1)}) custom-call(bf16[4,456,128]{2,1,0:T(8,128)(2,1)} %get-tuple-element.6.field_ref, bf16[4,456,128]{2,1,0:T(8,128)(2,1)} %get-tuple-element.7.corr_ref), custom_call_target="tpu_custom_call" | custom-call | tf_op jit(solution)/shard_map/pallas_call | solution.py:512

commit v6 on v5

--- a/solution.py
+++ b/solution.py
@@ -194,11 +194,11 @@
         pad_operator(o)
         return carry
 
-    lax.fori_loop(0, nops // 2, pad_some, 0)
+    lax.fori_loop(0, nops // 4, pad_some, 0)
     for j in range(1, ns):
         relay_boxes(0, j)
-        if j in (9, 17):
-            lax.fori_loop(nops // 2 + (j - 9) // 2, nops // 2 + (j - 9) // 2 + nops // 4, pad_some, 0)
+        if j % 2 == 0 and j <= 3 * nops // 2:
+            pad_operator(nops // 4 + j // 2 - 1)
 
     loads[2].wait()
     for own in owns:
@@ -429,15 +429,21 @@
         corr_ref[c] = dot_nt(eye, total.astype(BF)).astype(BF)
 
 
-def hand_over(field_ref, corr_ref, field_out, corr_out, sem):
-    copies = [
-        pltpu.make_async_copy(field_ref, field_out, sem.at[0]),
-        pltpu.make_async_copy(corr_ref, corr_out, sem.at[1]),
-    ]
-    for copy in copies:
-        copy.start()
-    for copy in copies:
-        copy.wait()
+def hand_over(field_ref, corr_ref, field_out, corr_out, held, load_sem, store_sem):
+    share = field_ref.shape[0]
+    loads, stores = [], []
+    for w, (source, target) in enumerate(((field_ref, field_out), (corr_ref, corr_out))):
+        for c in range(share):
+            place = held.at[w, c]
+            loads.append(pltpu.make_async_copy(source.at[c], place, load_sem.at[w, c]))
+            stores.append(pltpu.make_async_copy(place, target.at[c], store_sem.at[w, c]))
+    for load in loads:
+        load.start()
+    for load, store in zip(loads, stores):
+        load.wait()
+        store.start()
+    for store in stores:
+        store.wait()
 
 
 def body(density, export_ids, list_slot, translations, patch_points, inverses):
@@ -512,9 +518,9 @@
     field, corrected = pl.pallas_call(
         hand_over,
         out_shape=(out, out),
-        in_specs=[vmem, vmem],
+        in_specs=[anyspace, anyspace],
         out_specs=(anyspace, anyspace),
-        scratch_shapes=[dma((2,))],
+        scratch_shapes=[pltpu.VMEM((2, share, width, boxes), BF), dma((2, share)), dma((2, share))],
     )(field, corrected)
     return jnp.transpose(field, (2, 0, 1)), jnp.transpose(corrected, (2, 0, 1))
 

time: 73.1 us -> 73 us (level)
  no operation moved by 1% of the time
where the time goes in v6:
time: 73 us; the launch traced here: 72.8 us
  Pallas kernels  72 us (99%)
  between operations  0.8 us (1%)
    pallas_call x1, Pallas kernels, body(): pl.pallas_call(functools.partial(kernel, sizes), out_shape=(out, out), in...  70 us
    pallas_call x1, Pallas kernels, body(): pl.pallas_call(hand_over, out_shape=(out, out), in_specs=[anyspace, anysp...  2.05 us

profile of v6, /device:TPU:0, one launch (start us, length us, event | category | flops | bytes accessed | tf_op | source)
XLA Modules:
  0.0 72.8 jit_solution(1411241020560750350)
XLA Ops:
  0.6 70.0 %shard_map.77 = (bf16[4,456,128]{2,1,0:T(8,128)(2,1)}, bf16[4,456,128]{2,1,0:T(8,128)(2,1)}) custom-call(bf16[16,456,128]{2,1,0:T(8,128)(2,1)} %bitcast.7, s32[4,32]{1,0:T(4,128)} %bitcast.9, s32[64,128]{1,0:T(8,128)} %bitcast.8, bf16[16,456,456]{2,1,0:T(8,128)(2,1)} %trans_hbm.1, s32[8,1024]{1,0:T(8,128)} %pts_ref.1, bf16[8,1024,1024]{2,1,0:T(8,128)(2,1)} %inv_hbm.1), custom_call_target="tpu_custom_call" | custom-call | tf_op jit(solution)/shard_map/pallas_call | solution.py:465
  70.6 2.0 %shard_map.78 = (bf16[4,456,128]{2,1,0:T(8,128)(2,1)}, bf16[4,456,128]{2,1,0:T(8,128)(2,1)}) custom-call(bf16[4,456,128]{2,1,0:T(8,128)(2,1)} %get-tuple-element.6.field_ref, bf16[4,456,128]{2,1,0:T(8,128)(2,1)} %get-tuple-element.7.corr_ref), custom_call_target="tpu_custom_call" | custom-call | tf_op jit(solution)/shard_map/pallas_call | solution.py:518
